TPU v7x, 256 devices: a whole 4x4x8 slice. The times are simulated.
256 devices in a mesh: mem: 32 (over y, x, core), cell: 8 (over z).
Axes of the slice: x: 4, y: 4, z: 8, core: 2. Of those that a mesh axis runs over, the one named last changes fastest.
Arguments:
- prior_ensemble: bfloat16 [512, 2, 262144], P('mem', None, 'cell'), may hold values from -12 to 12
- measurement_location: int32 [32, 4096], P('cell', 'mem'), may hold values from 0 to 524287, as said below
- measurement_datum: float32 [32, 4096], P('cell', 'mem'), may hold values from -32 to 32
- measurement_spread: float32 [32, 4096], P('cell', 'mem'), may hold values from 1.2 to 20
Outputs:
- analysis: bfloat16 [512, 2, 262144], P('mem', None, 'cell')
Inputs may be any that keep to these rules, and one draw needn't show every extreme that they name: `measurement_location`: with v an entry at row r and column c, v // 262144 is its field and v % 262144 its cell; that cell is one of the 1024 cells that begin at ((r // 4) * 32 + c // 128) * 1024. Within each such block of 4 rows and 128 columns the entries are distinct, and they include the first cell of field 0 and the last cell of field 1 of that range.
All inputs are finite; a program needn't handle non-finite values.
Results may differ from a plain program's by a relative error of at most 0.0063.
Values may be sent and summed in bfloat16 or wider, within the bound.
No kernel may reach another device: no remote copies, remote signals or barrier semaphores. Data moves between devices by JAX's collectives and lax.ppermute only.
A program may use at most 64 MiB of HBM per device.

v0:
```python
import math

import jax
import jax.numpy as jnp
from jax import lax
from jax.sharding import Mesh
from jax.sharding import PartitionSpec as P

NS_ITERS = 8
MEM = ("mem_0", "mem_1", "mem_2")


def cut_along(shard, dim, peers):
    before, after = (shard.shape[:dim], shard.shape[dim + 1 :])
    return jnp.moveaxis(shard.reshape(*before, peers, -1, *after), dim, 0)


def in_order(tiles, dim):
    lengths = list(tiles.shape[1:])
    lengths[dim] *= tiles.shape[0]
    return jnp.moveaxis(tiles, 0, dim).reshape(lengths)


def moved_by_axis(tiles, axes, sequence):
    inside = tiles.shape[1:]
    filled = tiles.reshape(*(lax.axis_size(a) for a in axes), *inside)
    for k in sequence:
        filled = lax.all_to_all(filled, axes[k], k, k, tiled=True)
    return filled.reshape(-1, *inside)


def core_and_chips(shard, groups, sequence, split_dim, concat_dim):
    peers = lax.axis_size(groups[0]) * lax.axis_size(groups[1])
    tiles = cut_along(shard, split_dim, peers)
    return in_order(moved_by_axis(tiles, groups, sequence), concat_dim)


def sent_together(arrays, axis, dim, along):
    widths = [math.prod(a.shape[along:]) for a in arrays]
    both = jnp.concatenate(
        [a.reshape(*a.shape[:along], w) for a, w in zip(arrays, widths)], axis=along
    )
    filled = lax.psum_scatter(both, axis, scatter_dimension=dim, tiled=True)
    tiles = jnp.split(filled, [sum(widths[:k]) for k in range(1, len(widths))], axis=along)
    return tuple(
        (b.reshape(*filled.shape[:along], *a.shape[along:]) for a, b in zip(arrays, tiles))
    )


def sent_to_all(shard, axis):
    peers = lax.axis_size(axis)
    return lax.all_to_all(
        jnp.broadcast_to(shard[None], (peers, *shard.shape)), axis, 0, 0, tiled=True
    )


def of_everyone(shard, axis):
    everything = sent_to_all(shard, axis)
    return jnp.sum(everything, axis=0)


def packed_total(arrays, axis):
    ends = [0]
    for a in arrays:
        ends.append(ends[-1] + a.size)
    subtotal = of_everyone(jnp.concatenate([a.ravel() for a in arrays]), axis)
    return tuple((subtotal[b:e].reshape(a.shape) for a, b, e in zip(arrays, ends, ends[1:])))


def gather_directly(shard, axis, dim):
    tiles = sent_to_all(shard, axis)
    return in_order(tiles, dim)


def local(prior_ensemble, measurement_location, measurement_datum, measurement_spread):
    highest = lax.Precision.HIGHEST
    gathered_lines = core_and_chips(prior_ensemble, (("mem_0", "mem_1"), "mem_2"), (1, 0), 2, 0)
    ensemble_size, fields, cell_dev = gathered_lines.shape
    norm_factor = math.sqrt(ensemble_size - 1)
    flat_state = gathered_lines.reshape(ensemble_size, fields * cell_dev)
    mean_state = jnp.sum(flat_state, axis=0, dtype=jnp.float32) / ensemble_size
    anomalies = (flat_state - mean_state).astype(jnp.bfloat16)
    grid_site_number = prior_ensemble.shape[2] * lax.axis_size("cell")
    block_start = (lax.axis_index("cell") * lax.axis_size(MEM) + lax.axis_index(MEM)) * cell_dev
    cell_ids = measurement_location.reshape(-1)
    local_slots = cell_ids // grid_site_number * cell_dev + (
        cell_ids % grid_site_number - block_start
    )
    errors = measurement_spread.reshape(-1)
    picked_lines = jnp.take(anomalies, local_slots, axis=1)
    scaled = (picked_lines.astype(jnp.float32) / (errors * norm_factor)).astype(jnp.bfloat16)
    innovation = (
        (measurement_datum.reshape(-1) - jnp.take(mean_state, local_slots)) / errors
    ).astype(jnp.bfloat16)
    gram_part = lax.dot_general(
        scaled, scaled, (((1,), (1,)), ((), ())), preferred_element_type=jnp.float32
    )
    proj_part = jnp.dot(
        scaled.astype(jnp.float32), innovation.astype(jnp.float32), precision=highest
    )
    row_count = ensemble_size // lax.axis_size(MEM)
    row_start = lax.axis_index(MEM) * row_count
    column_iota = lax.broadcasted_iota(jnp.int32, (row_count, ensemble_size), 1)
    row_iota = lax.broadcasted_iota(jnp.int32, (row_count, ensemble_size), 0)
    eye_rows = (column_iota == row_iota + row_start).astype(jnp.float32)
    identity = jnp.eye(ensemble_size, dtype=jnp.float32)
    gram_rows, proj_rows = sent_together((gram_part, proj_part), MEM, 0, 1)
    gram_rows, proj_rows = packed_total((gram_rows, proj_rows), "cell")
    system_rows = gram_rows + eye_rows
    placed = lax.dynamic_update_slice_in_dim(
        jnp.zeros((ensemble_size,), jnp.float32), proj_rows, row_start, 0
    )
    square_sum, projected = packed_total((jnp.sum(system_rows * system_rows), placed), MEM)
    norm_scale = jnp.sqrt(square_sum)
    whole_system = gather_directly(system_rows, MEM, 0)

    def whole_turn(turn, pair):
        whole_y, whole_z = pair
        newton_step = 1.5 * identity - 0.5 * jnp.dot(whole_z, whole_y, precision=highest)
        return (
            jnp.dot(newton_step, whole_y, precision=highest),
            jnp.dot(newton_step, whole_z, precision=highest),
        )

    whole_y, whole_z = lax.fori_loop(0, NS_ITERS, whole_turn, (whole_system / norm_scale, identity))
    iterate_z = lax.dynamic_slice_in_dim(whole_z, row_start, row_count, 0)
    divisor = jnp.sqrt(norm_scale) * norm_factor
    vector_z = jnp.dot(whole_z, projected, precision=highest)
    shift_weights = vector_z / divisor
    weight_rows = (iterate_z / jnp.sqrt(norm_scale)).astype(jnp.bfloat16)
    updated = jnp.dot(
        gather_directly(weight_rows, MEM, 0), anomalies, preferred_element_type=jnp.float32
    )
    mean_shift = jnp.dot(shift_weights, updated, precision=highest)
    analysis = (
        (mean_state + mean_shift + updated)
        .astype(jnp.bfloat16)
        .reshape(ensemble_size, fields, cell_dev)
    )
    return lax.all_to_all(analysis, MEM, split_axis=0, concat_axis=2, tiled=True)


def solution(mesh):
    torus = Mesh(
        mesh.devices.reshape(4, 4, 2, mesh.shape["cell"]), ("mem_0", "mem_1", "mem_2", "cell")
    )
    in_specs = (P(MEM, None, "cell"), P("cell", MEM), P("cell", MEM), P("cell", MEM))
    out_specs = P(MEM, None, "cell")
    return jax.shard_map(local, mesh=torus, in_specs=in_specs, out_specs=out_specs, check_vma=False)
```

profile of v0, /device:TPU:1, one launch (start us, length us, event | category | flops | bytes accessed | tf_op | source)
XLA Modules:
  0.0 339.8 jit_solution(10988353108218990096)
XLA Ops:
  6.5 3.3 reshape.259
  9.8 1.2 copy.45
  11.0 2.2 copy.46
  13.2 8.2 %all_to_all.50 = bf16[16,2,16,2,1024]{4,3,2,0,1:T(2,128)(2,1)S(1)} all-to-all(bf16[16,2,16,2,1024]{4,3,2,0,1:T(2,128)(2,1)S(1)} %copy.46), channel_id=1, replica_groups=mesh['mem_0'=4,'mem_1'=4,'mem_2'=2,'cell'=8] {'mem_2'}, dimensions={1} | all-to-all | bytes 4194304 | tf_op jit(solution)/shard_map/all_to_all | solution.py:28
  21.4 3.0 copy.47
  24.5 5.2 %all-to-all-start.1 = ((bf16[16,2,16,2,1024]{4,3,2,1,0:T(2,128)(2,1)}), bf16[16,2,16,2,1024]{4,3,2,1,0:T(2,128)(2,1)S(1)}, u32[]{:S(2)}, u32[]{:S(2)}) async-start(bf16[16,2,16,2,1024]{4,3,2,1,0:T(2,128)(2,1)} %copy.47), calls=%async_computation.1 | async-start | bytes 4194304 | tf_op jit(solution)/shard_map/all_to_all | solution.py:28
  29.8 32.0 %all-to-all-done.1 = bf16[16,2,16,2,1024]{4,3,2,1,0:T(2,128)(2,1)S(1)} async-done(((bf16[16,2,16,2,1024]{4,3,2,1,0:T(2,128)(2,1)}), bf16[16,2,16,2,1024]{4,3,2,1,0:T(2,128)(2,1)S(1)}, u32[]{:S(2)}, u32[]{:S(2)}) %all-to-all-start.1) | async-done | bytes 2097184 | tf_op jit(solution)/shard_map/all_to_all | solution.py:28
  61.8 1.7 convert_reduce_fusion
  63.5 2.7 copy.66
  66.2 5.4 %copy.48 = f32[512,2048]{0,1:T(8,128)} copy(f32[512,2048]{1,0:T(8,128)} %bitcast.108) | data formatting | bytes 8388608 | tf_op jit(solution)/shard_map/convert_element_type | solution.py:81
  71.6 3.1 gather_fusion.1
  74.7 2.5 subtract_convert_fusion.1
  77.3 2.0 gather_fusion
  80.3 1.5 copy.55
  81.8 84.7 %reduce-scatter.4.cloned.1.call-done = f32[16,513]{1,0:T(8,128)} async-done(((f32[512,513]{1,0:T(8,128)}), f32[16,513]{1,0:T(8,128)}) %reduce-scatter.4.cloned.1.call-update) | async-done | bytes 32848
  166.5 0.8 slice_bitcast_fusion
  167.2 0.7 split.9
  168.0 0.8 broadcast_in_dim.29
  168.9 6.8 %all-to-all-start.2 = ((f32[8,1,8208]{2,1,0:T(1,128)}), f32[8,1,8208]{2,1,0:T(1,128)S(1)}, u32[]{:S(2)}, u32[]{:S(2)}) async-start(f32[8,1,8208]{2,1,0:T(1,128)} %broadcast_in_dim.29), calls=%async_computation.2 | async-start | bytes 532480 | tf_op jit(solution)/shard_map/all_to_all | solution.py:52
  175.7 9.4 %all-to-all-done.2 = f32[8,1,8208]{2,1,0:T(1,128)S(1)} async-done(((f32[8,1,8208]{2,1,0:T(1,128)}), f32[8,1,8208]{2,1,0:T(1,128)S(1)}, u32[]{:S(2)}, u32[]{:S(2)}) %all-to-all-start.2) | async-done | bytes 262688 | tf_op jit(solution)/shard_map/all_to_all | solution.py:52
  185.3 0.7 multiply_reduce_fusion
  186.1 0.8 pad_maximum_fusion.2
  186.9 0.7 broadcast_in_dim.52
  187.5 8.7 %all-to-all-start.4 = ((f32[32,1,513]{2,1,0:T(1,128)}), f32[32,1,513]{2,1,0:T(1,128)S(1)}, u32[]{:S(2)}, u32[]{:S(2)}) async-start(f32[32,1,513]{2,1,0:T(1,128)} %broadcast_in_dim.52), calls=%async_computation.4 | async-start | bytes 163840 | tf_op jit(solution)/shard_map/all_to_all | solution.py:52
  196.3 7.3 %all-to-all-done.4 = f32[32,1,513]{2,1,0:T(1,128)S(1)} async-done(((f32[32,1,513]{2,1,0:T(1,128)}), f32[32,1,513]{2,1,0:T(1,128)S(1)}, u32[]{:S(2)}, u32[]{:S(2)}) %all-to-all-start.4) | async-done | bytes 65696 | tf_op jit(solution)/shard_map/all_to_all | solution.py:52
  203.6 1.1 broadcast_in_dim.50
  204.7 4.0 %all-to-all-start.3 = ((f32[32,16,512]{2,1,0:T(8,128)}), f32[32,16,512]{2,1,0:T(8,128)S(1)}, u32[]{:S(2)}, u32[]{:S(2)}) async-start(f32[32,16,512]{2,1,0:T(8,128)} %broadcast_in_dim.50), calls=%async_computation.3 | async-start | bytes 2097152 | tf_op jit(solution)/shard_map/all_to_all | solution.py:52
  210.2 15.7 %all-to-all-done.3 = f32[32,16,512]{2,1,0:T(8,128)S(1)} async-done(((f32[32,16,512]{2,1,0:T(8,128)}), f32[32,16,512]{2,1,0:T(8,128)S(1)}, u32[]{:S(2)}, u32[]{:S(2)}) %all-to-all-start.3) | async-done | bytes 1048608 | tf_op jit(solution)/shard_map/all_to_all | solution.py:52
  226.0 45.9 %while.13 = (s32[]{:T(128)}, f32[512,512]{1,0:T(8,128)S(1)}, f32[512,512]{1,0:T(8,128)S(1)}, s32[]{:T(128)}) while((s32[]{:T(128)}, f32[512,512]{1,0:T(8,128)S(1)}, f32[512,512]{1,0:T(8,128)S(1)}, s32[]{:T(128)}) %tuple.30), condition=%wide.region_6.7_spmd.clone, body=%wide.region_5.6_spmd.clone.sunk | while | flops 4832886784 | bytes 13631541 | solution.py:125
  226.2 1.9 fusion.53
  228.0 1.8 fusion.55
  229.9 1.8 fusion.54
  231.9 1.8 fusion.53
  233.8 1.8 fusion.55
  235.6 1.8 fusion.54
  237.6 1.9 fusion.53
  239.5 1.8 fusion.55
  241.3 1.8 fusion.54
  243.4 1.8 fusion.53
  245.2 1.8 fusion.55
  247.1 1.8 fusion.54
  249.1 1.9 fusion.53
  251.0 1.8 fusion.55
  252.8 1.8 fusion.54
  254.8 1.8 fusion.53
  256.7 1.8 fusion.55
  258.6 1.8 fusion.54
  260.6 1.9 fusion.53
  262.4 1.8 fusion.55
  264.3 1.8 fusion.54
  266.3 1.8 fusion.53
  268.2 1.8 fusion.55
  270.0 1.8 fusion.54
  271.9 0.9 broadcast_in_dim.53
  272.8 4.6 %all-to-all-start.5 = ((bf16[32,16,512]{2,1,0:T(8,128)(2,1)}), bf16[32,16,512]{2,1,0:T(8,128)(2,1)}, u32[]{:S(2)}, u32[]{:S(2)}) async-start(bf16[32,16,512]{2,1,0:T(8,128)(2,1)} %broadcast_in_dim.53), calls=%async_computation.5 | async-start | bytes 1048576 | tf_op jit(solution)/shard_map/all_to_all | solution.py:52
  277.4 3.7 %subtract_convert_fusion = bf16[16,2,16,2,1024]{4,3,2,1,0:T(2,128)(2,1)S(1)} fusion(f32[2,1024]{1,0:T(2,128)S(1)} %get-tuple-element.46, bf16[16,2,16,2,1024]{4,3,2,1,0:T(2,128)(2,1)} %copy-done), kind=kLoop, calls=%fused_computation.7 | loop fusion | flops 3145728 | bytes 4202496 | tf_op jit(solution)/shard_map/convert_element_type | solution.py:82
  281.8 1.0 fusion.20
  282.8 6.2 %all-to-all-done.5 = bf16[32,16,512]{2,1,0:T(8,128)(2,1)} async-done(((bf16[32,16,512]{2,1,0:T(8,128)(2,1)}), bf16[32,16,512]{2,1,0:T(8,128)(2,1)}, u32[]{:S(2)}, u32[]{:S(2)}) %all-to-all-start.5) | async-done | bytes 524320 | tf_op jit(solution)/shard_map/all_to_all | solution.py:52
  289.0 2.3 fusion.21
  291.3 2.1 fusion.22
  293.9 2.8 reshape.234
  296.6 32.4 %all_to_all.51 = bf16[512,2,1024]{2,1,0:T(2,128)(2,1)S(1)} all-to-all(bf16[512,2,1024]{2,1,0:T(2,128)(2,1)} %reshape.234), channel_id=1, replica_groups=mesh['mem_0'=4,'mem_1'=4,'mem_2'=2,'cell'=8] {'mem_0','mem_1','mem_2'}, dimensions={0} | all-to-all | bytes 4194304 | tf_op jit(solution)/shard_map/all_to_all | solution.py:140
  329.1 1.2 copy.74
  330.2 2.8 all_to_all.42
  (57 shorter events, 4.9 us)
Async XLA Ops:
  24.5 5.3 %copy-start.1 = (s32[4,128]{1,0:T(4,128)S(1)}, s32[4,128]{1,0:T(4,128)}, u32[]{:S(2)}) copy-start(s32[4,128]{1,0:T(4,128)} %param.7) | copy-start | bytes 6148
  24.5 37.3 %all-to-all-start.1 = ((bf16[16,2,16,2,1024]{4,3,2,1,0:T(2,128)(2,1)}), bf16[16,2,16,2,1024]{4,3,2,1,0:T(2,128)(2,1)S(1)}, u32[]{:S(2)}, u32[]{:S(2)}) async-start(bf16[16,2,16,2,1024]{4,3,2,1,0:T(2,128)(2,1)} %copy.47), calls=%async_computation.1 | async-start | bytes 4194304 | tf_op jit(solution)/shard_map/all_to_all | solution.py:28
  29.7 136.8 %reduce-scatter.4.cloned.1.call-start = ((), (), s32[]{:S(2)}) async-start(), calls=%async_computation.8 | async-start | bytes 1351680
  61.8 4.4 %copy-start = (bf16[16,2,16,2,1024]{4,3,2,1,0:T(2,128)(2,1)}, bf16[16,2,16,2,1024]{4,3,2,1,0:T(2,128)(2,1)S(1)}, u32[]{:S(2)}) copy-start(bf16[16,2,16,2,1024]{4,3,2,1,0:T(2,128)(2,1)S(1)} %all-to-all-done.1) | copy-start | bytes 6291460
  77.2 2.0 copy-start.2
  77.3 2.0 copy-start.3
  168.9 16.2 %all-to-all-start.2 = ((f32[8,1,8208]{2,1,0:T(1,128)}), f32[8,1,8208]{2,1,0:T(1,128)S(1)}, u32[]{:S(2)}, u32[]{:S(2)}) async-start(f32[8,1,8208]{2,1,0:T(1,128)} %broadcast_in_dim.29), calls=%async_computation.2 | async-start | bytes 532480 | tf_op jit(solution)/shard_map/all_to_all | solution.py:52
  187.5 16.1 %all-to-all-start.4 = ((f32[32,1,513]{2,1,0:T(1,128)}), f32[32,1,513]{2,1,0:T(1,128)S(1)}, u32[]{:S(2)}, u32[]{:S(2)}) async-start(f32[32,1,513]{2,1,0:T(1,128)} %broadcast_in_dim.52), calls=%async_computation.4 | async-start | bytes 163840 | tf_op jit(solution)/shard_map/all_to_all | solution.py:52
  204.7 21.1 %all-to-all-start.3 = ((f32[32,16,512]{2,1,0:T(8,128)}), f32[32,16,512]{2,1,0:T(8,128)S(1)}, u32[]{:S(2)}, u32[]{:S(2)}) async-start(f32[32,16,512]{2,1,0:T(8,128)} %broadcast_in_dim.50), calls=%async_computation.3 | async-start | bytes 2097152 | tf_op jit(solution)/shard_map/all_to_all | solution.py:52
  272.8 16.2 %all-to-all-start.5 = ((bf16[32,16,512]{2,1,0:T(8,128)(2,1)}), bf16[32,16,512]{2,1,0:T(8,128)(2,1)}, u32[]{:S(2)}, u32[]{:S(2)}) async-start(bf16[32,16,512]{2,1,0:T(8,128)(2,1)} %broadcast_in_dim.53), calls=%async_computation.5 | async-start | bytes 1048576 | tf_op jit(solution)/shard_map/all_to_all | solution.py:52
Sparse Core Ops, SparseCore 0:
  81.9 84.4 reduce-scatter.3
where the time goes:
time: 341 us; the launch traced here: 340 us
  waiting for transfers between devices  155 us (45%)
  matrix products  50.4 us (15%)
  blocking collectives  40.7 us (12%)
  local copies, waits for them, and re-layouts  38.5 us (11%)
  starting transfers between devices  29.3 us (9%)
  between operations  14.4 us (4%)
  other arithmetic  10.9 us (3%)
    unnamed x2, waiting for transfers between devices  84.7 us
    all_to_all x4, waiting for transfers between devices, sent_to_all(): lax.all_to_all(jnp.broadcast_to(shard[None], (peers, *shard.shape)), axis...  38.5 us
    all_to_all x1, blocking collectives, local(): lax.all_to_all(analysis, MEM, split_axis=0, concat_axis=2, tiled=True)  32.4 us
    all_to_all x1, waiting for transfers between devices, moved_by_axis(): filled = lax.all_to_all(filled, axes[k], k, k, tiled=True)  32 us
    all_to_all x4, starting transfers between devices, sent_to_all(): lax.all_to_all(jnp.broadcast_to(shard[None], (peers, *shard.shape)), axis...  24.1 us
    dot_general x8, matrix products, whole_turn(): jnp.dot(whole_z, whole_y, precision=highest)  14.8 us
    dot_general x8, matrix products, whole_turn(): jnp.dot(newton_step, whole_y, precision=highest)  14.8 us
    dot_general x8, matrix products, whole_turn(): jnp.dot(newton_step, whole_z, precision=highest)  14.8 us
  transfers between devices with their start and end apart: 6, of which 6 were waited for; matrix products, arithmetic and copies ran while one was open for 2% of the time, Pallas kernels for 0%

commit v1 on v0

v1 whole, which is shorter than its diff:
```python
import functools
import math

import jax
import jax.numpy as jnp
from jax import lax
from jax.experimental import pallas as pl
from jax.experimental.pallas import tpu as pltpu
from jax.sharding import Mesh
from jax.sharding import PartitionSpec as P

NS_ITERS = 8
MEM = ("mem_0", "mem_1", "mem_2")
CHIPS = ("mem_0", "mem_1", "cell")
F32 = jnp.float32
BF16 = jnp.bfloat16
VMEM = pl.BlockSpec(memory_space=pltpu.VMEM)
SMEM = pl.BlockSpec(memory_space=pltpu.SMEM)
ANY = pl.BlockSpec(memory_space=pl.ANY)


def pack_kernel(x_ref, o_ref, sem):
    blocks, width = o_ref.shape[0], o_ref.shape[3]
    copies = [
        pltpu.make_async_copy(
            x_ref.at[:, :, pl.ds(b * width, width)], o_ref.at[b], sem.at[b]
        )
        for b in range(blocks)
    ]
    for c in copies:
        c.start()
    for c in copies:
        c.wait()


def unpack_kernel(x_ref, o_ref, sem):
    blocks, width = x_ref.shape[0], x_ref.shape[3]
    copies = [
        pltpu.make_async_copy(
            x_ref.at[b], o_ref.at[:, :, pl.ds(b * width, width)], sem.at[b]
        )
        for b in range(blocks)
    ]
    for c in copies:
        c.start()
    for c in copies:
        c.wait()


def rows_of(x_ref, f):
    groups, _, eight, width = x_ref.shape
    return x_ref[:, f].reshape(groups * eight, width)


def contract(a, b, dims):
    return lax.dot_general(a, b, (dims, ((), ())), preferred_element_type=F32)


def gram_kernel(core_ref, slot_ref, datum_ref, spread_ref, x_ref, keep_ref, send_ref, gram_ref):
    groups, fields, eight, width = x_ref.shape
    members = groups * eight
    norm_factor = math.sqrt(members - 1)
    scaled_parts, innovation_parts = [], []
    iota = lax.broadcasted_iota(jnp.int32, (width, 128), 0)
    for r in range(slot_ref.shape[0]):
        slot = slot_ref[r : r + 1, :]
        picked = None
        for f in range(fields):
            chosen = jnp.where(iota == slot - f * width, 1.0, 0.0).astype(BF16)
            term = contract(rows_of(x_ref, f), chosen, ((1,), (0,)))
            picked = term if picked is None else picked + term
        mean = jnp.sum(picked, axis=0, keepdims=True) / members
        anomaly = (picked - mean).astype(BF16).astype(F32)
        error = spread_ref[r : r + 1, :]
        scaled_parts.append((anomaly / (error * norm_factor)).astype(BF16))
        innovation_parts.append(((datum_ref[r : r + 1, :] - mean) / error).astype(BF16))
    scaled = jnp.concatenate(scaled_parts, axis=1)
    innovation = jnp.concatenate(innovation_parts, axis=1).astype(F32)
    innovation = jnp.broadcast_to(innovation, (16, innovation.shape[1])).astype(BF16)
    gram_ref[...] = contract(scaled, scaled, ((1,), (1,)))
    projected = contract(innovation, scaled, ((1,), (1,)))
    for j in range(members // 128):
        gram_ref[members - 8 + j : members - 7 + j, 0:128] = projected[0:1, j * 128 : (j + 1) * 128]
    half = members // 2
    lanes = members // 128
    core = core_ref[0]
    for part, ref in ((core, keep_ref), (1 - core, send_ref)):
        start = pl.multiple_of(part * half, half)
        rows = gram_ref[pl.ds(start, half), :]
        for i in range(half // 8):
            for j in range(lanes):
                ref[i * lanes + j] = rows[i * 8 : i * 8 + 8, j * 128 : j * 128 + 128]


def mean_kernel(x_ref, anomalies_ref, mean_ref):
    groups, fields, eight, width = x_ref.shape
    members = groups * eight
    for f in range(fields):
        x = x_ref[:, f].astype(F32)
        mean = jnp.sum(jnp.sum(x, axis=0), axis=0, keepdims=True) / members
        mean_ref[f : f + 1, :] = mean
        anomalies_ref[:, f] = (x - mean[None]).astype(BF16)


def halves(a):
    high = a.astype(BF16)
    return high, (a - high.astype(F32)).astype(BF16)


def thirds(row):
    high = row.astype(BF16).astype(F32)
    rest = row - high
    middle = rest.astype(BF16).astype(F32)
    low = rest - middle
    pad = jnp.zeros((13, row.shape[1]), F32)
    return jnp.concatenate([high, middle, low, pad], axis=0).astype(BF16)


def times(a, b):
    dims = ((1,), (0,))
    return contract(a[0], b[0], dims) + (contract(a[0], b[1], dims) + contract(a[1], b[0], dims))


def analysis_kernel(core_ref, own_ref, other_ref, anomalies_ref, mean_ref, o_ref, sys_ref, yh, yl, zh, zl, zf):
    members = sys_ref.shape[0]
    norm_factor = math.sqrt(members - 1)
    half, lanes = members // 2, members // 128
    core = core_ref[0]
    for part, ref in ((core, own_ref), (1 - core, other_ref)):
        start = pl.multiple_of(part * half, half)
        for i in range(half // 8):
            for j in range(lanes):
                sys_ref[pl.ds(start + i * 8, 8), j * 128 : (j + 1) * 128] = ref[i * lanes + j]
    tile = sys_ref[members - 8 : members, 0:128]
    projected = jnp.concatenate([tile[j : j + 1, :] for j in range(lanes)], axis=1)
    mirror = jnp.transpose(sys_ref[0:128, members - 128 : members])
    sys_ref[members - 8 : members, 0:128] = mirror[120:128, :]
    row_iota = lax.broadcasted_iota(jnp.int32, (members, members), 0)
    column_iota = lax.broadcasted_iota(jnp.int32, (members, members), 1)
    diagonal = row_iota == column_iota
    system = sys_ref[...] + jnp.where(diagonal, 1.0, 0.0)
    squares = jnp.sum(jnp.sum(system * system, axis=0, keepdims=True), axis=1, keepdims=True)
    norm_scale = jnp.sqrt(squares)
    start_y = system / norm_scale

    def step_of(product):
        return jnp.where(diagonal, 1.5, 0.0) - 0.5 * product

    first = step_of(start_y)
    first_parts = halves(first)
    zh[...], zl[...] = first_parts
    yh[...], yl[...] = halves(times(first_parts, halves(start_y)))

    def turn(_, carry):
        y, z = (yh[...], yl[...]), (zh[...], zl[...])
        step = halves(step_of(times(z, y)))
        yh[...], yl[...] = halves(times(step, y))
        zh[...], zl[...] = halves(times(step, z))
        return carry

    lax.fori_loop(0, NS_ITERS - 2, turn, 0)
    z = (zh[...], zl[...])
    step = halves(step_of(times(z, (yh[...], yl[...]))))
    zf[...] = times(step, z)
    iterate_z = zf[...]
    root = jnp.sqrt(norm_scale)
    dims = ((1,), (0,))
    z = halves(iterate_z)
    three = thirds(projected)
    sent = contract(three, z[0], dims) + contract(three, z[1], dims)
    shift = jnp.sum(sent, axis=0, keepdims=True) / (root * norm_factor)
    weights = (iterate_z / root).astype(BF16)
    combined = jnp.sum(contract(thirds(shift), weights, dims), axis=0, keepdims=True)
    combined = thirds(combined)
    groups, fields, eight, width = anomalies_ref.shape
    for f in range(fields):
        anomalies = rows_of(anomalies_ref, f)
        mean_shift = jnp.sum(contract(combined, anomalies, dims), axis=0, keepdims=True)
        base = mean_ref[f : f + 1, :] + mean_shift
        updated = contract(weights, anomalies, dims)
        o_ref[:, f] = (base + updated).astype(BF16).reshape(groups, eight, width)


def shape(dims, dtype):
    return jax.ShapeDtypeStruct(dims, dtype)


def local(prior_ensemble, measurement_location, measurement_datum, measurement_spread):
    rows, fields, span = prior_ensemble.shape
    peers = lax.axis_size(MEM)
    members = rows * peers
    width = span // peers
    core = lax.axis_index("mem_2").reshape(1).astype(jnp.int32)
    packed = pl.pallas_call(
        pack_kernel,
        out_shape=shape((peers, rows, fields, width), BF16),
        in_specs=[ANY],
        out_specs=ANY,
        scratch_shapes=[pltpu.SemaphoreType.DMA((peers,))],
        name="pack",
    )(prior_ensemble)
    gathered = lax.all_to_all(packed.reshape(members, fields, width), MEM, 0, 0, tiled=True)
    groups = members // 8
    state = gathered.reshape(groups, 8, fields, width).transpose(0, 2, 1, 3)
    sites = span * lax.axis_size("cell")
    block_start = (lax.axis_index("cell") * peers + lax.axis_index(MEM)) * width
    slots = measurement_location // sites * width + (measurement_location % sites - block_start)
    chips = lax.axis_size(CHIPS)
    tiles = shape((chips, 8, 128), F32)
    keep, send = pl.pallas_call(
        gram_kernel,
        out_shape=(tiles, tiles),
        in_specs=[SMEM, VMEM, VMEM, VMEM, VMEM],
        out_specs=(VMEM, VMEM),
        scratch_shapes=[pltpu.VMEM((members, members), F32)],
        name="gram",
    )(core, slots, measurement_datum, measurement_spread, state)
    swap = [(0, 1), (1, 0)]
    part = keep + lax.ppermute(send, "mem_2", swap)
    part = lax.all_to_all(part, CHIPS, 0, 0, tiled=True)
    total = jnp.broadcast_to(jnp.sum(part, axis=0, keepdims=True), part.shape)
    own = lax.all_to_all(total, CHIPS, 0, 0, tiled=True)
    other = lax.ppermute(own, "mem_2", swap)
    anomalies, mean = pl.pallas_call(
        mean_kernel,
        out_shape=(shape(state.shape, BF16), shape((fields, width), F32)),
        in_specs=[VMEM],
        out_specs=(VMEM, VMEM),
        name="mean",
    )(state)
    square = pltpu.VMEM((members, members), BF16)
    whole = pltpu.VMEM((members, members), F32)
    analysis = pl.pallas_call(
        analysis_kernel,
        out_shape=shape(state.shape, BF16),
        in_specs=[SMEM, VMEM, VMEM, VMEM, VMEM],
        out_specs=VMEM,
        scratch_shapes=[whole, square, square, square, square, whole],
        name="analysis",
    )(core, own, other, anomalies, mean)
    analysis = analysis.transpose(0, 2, 1, 3).reshape(members, fields, width)
    returned = lax.all_to_all(analysis, MEM, 0, 0, tiled=True)
    return pl.pallas_call(
        unpack_kernel,
        out_shape=shape(prior_ensemble.shape, BF16),
        in_specs=[ANY],
        out_specs=ANY,
        scratch_shapes=[pltpu.SemaphoreType.DMA((peers,))],
        name="unpack",
    )(returned.reshape(peers, rows, fields, width))


def solution(mesh):
    torus = Mesh(
        mesh.devices.reshape(4, 4, 2, mesh.shape["cell"]), ("mem_0", "mem_1", "mem_2", "cell")
    )
    in_specs = (P(MEM, None, "cell"), P("cell", MEM), P("cell", MEM), P("cell", MEM))
    out_specs = P(MEM, None, "cell")
    return jax.shard_map(local, mesh=torus, in_specs=in_specs, out_specs=out_specs, check_vma=False)
```

time: 341 us -> 303 us (0.89)
  Pallas kernels: 0 us -> 163 us
  waiting for transfers between devices: 155 us -> 29.7 us
  matrix products: 50.4 us -> 0 us
  blocking collectives: 40.7 us -> 87.7 us
  local copies, waits for them, and re-layouts: 38.5 us -> 6.7 us
  starting transfers between devices: 29.3 us -> 13.2 us
  between operations: 14.4 us -> 0.23 us
  other arithmetic: 10.9 us -> 1.85 us
    pallas_call x0 -> x5, Pallas kernels: none -> 163 us  [the longest x1 64.9 us: local(): pl.pallas_call(unpack_kernel, out_shape=shape(prior_ensemble.shape, BF16)...]
    unnamed x2 -> x0, waiting for transfers between devices: 84.7 us -> none
    dot_general x29 -> x0, matrix products: 50.4 us -> none  [the longest x8 14.8 us: whole_turn(): jnp.dot(whole_z, whole_y, precision=highest)]
    all_to_all x2 -> x3, blocking collectives: 40.7 us -> 87.7 us  [the longest x1 31.9 us: local(): returned = lax.all_to_all(analysis, MEM, 0, 0, tiled=True)]
    all_to_all x5 -> x1, waiting for transfers between devices: 70.5 us -> 28 us  [local(): lax.all_to_all(packed.reshape(members, fields, width), MEM, 0, 0, tiled=T...]
    all_to_all x5 -> x1, starting transfers between devices: 29.3 us -> 8.59 us  [local(): lax.all_to_all(packed.reshape(members, fields, width), MEM, 0, 0, tiled=T...]
    convert_element_type x7 -> x0, other arithmetic: 7.08 us -> none  [the longest x2 6.22 us: local(): anomalies = (flat_state - mean_state).astype(jnp.bfloat16)]
    all_to_all x3 -> x0, local copies, waits for them, and re-layouts: 6.95 us -> none  [the longest x2 3.91 us: local(): lax.all_to_all(analysis, MEM, split_axis=0, concat_axis=2, tiled=True)]
  transfers between devices with their start and end apart: 6 -> 3, of which waited for: 6 -> 2; matrix products, arithmetic and copies ran while one was open for 2% -> 0% of each run, Pallas kernels for 0% -> 1%
where the time goes in v1:
time: 303 us; the launch traced here: 302 us
  Pallas kernels  163 us (54%)
  blocking collectives  87.7 us (29%)
  waiting for transfers between devices  29.7 us (10%)
  starting transfers between devices  13.2 us (4%)
  local copies, waits for them, and re-layouts  6.7 us (2%)
    pallas_call x1, Pallas kernels, local(): pl.pallas_call(unpack_kernel, out_shape=shape(prior_ensemble.shape, BF16)...  64.9 us
    pallas_call x1, Pallas kernels, local(): pl.pallas_call(pack_kernel, out_shape=shape((peers, rows, fields, width),...  64.9 us
    all_to_all x1, blocking collectives, local(): returned = lax.all_to_all(analysis, MEM, 0, 0, tiled=True)  31.9 us
    all_to_all x1, blocking collectives, local(): part = lax.all_to_all(part, CHIPS, 0, 0, tiled=True)  31 us
    all_to_all x1, waiting for transfers between devices, local(): lax.all_to_all(packed.reshape(members, fields, width), MEM, 0, 0, tiled=T...  28 us
    all_to_all x1, blocking collectives, local(): own = lax.all_to_all(total, CHIPS, 0, 0, tiled=True)  24.8 us
    pallas_call x1, Pallas kernels, local(): pl.pallas_call(analysis_kernel, out_shape=shape(state.shape, BF16), in_sp...  24 us
    all_to_all x1, starting transfers between devices, local(): lax.all_to_all(packed.reshape(members, fields, width), MEM, 0, 0, tiled=T...  8.59 us
  transfers between devices with their start and end apart: 3, of which 2 were waited for; matrix products, arithmetic and copies ran while one was open for 0% of the time, Pallas kernels for 1%

profile of v1, /device:TPU:1, one launch (start us, length us, event | category | flops | bytes accessed | tf_op | source)
XLA Modules:
  0.0 302.5 jit_solution(4677191179611226407)
XLA Ops:
  0.0 64.9 %pack.1 = bf16[32,16,2,1024]{3,2,1,0:T(2,128)(2,1)} custom-call(bf16[16,2,32768]{2,1,0:T(2,128)(2,1)} %x_ref.1), custom_call_target="tpu_custom_call" | custom-call | tf_op jit(solution)/shard_map/pack/pallas_call | solution.py:194
  64.9 0.0 copy-start.2
  64.9 8.6 %all-to-all-start = ((bf16[512,2,1024]{2,1,0:T(2,128)(2,1)}), bf16[512,2,1024]{2,1,0:T(2,128)(2,1)S(1)}, u32[]{:S(2)}, u32[]{:S(2)}) async-start(bf16[512,2,1024]{2,1,0:T(2,128)(2,1)} %bitcast.15), calls=%async_computation | async-start | bytes 4194304 | tf_op jit(solution)/shard_map/all_to_all | solution.py:202
  73.5 0.0 copy-done.2
  73.6 0.6 fusion.1.slot_ref
  74.1 28.0 %all-to-all-done = bf16[512,2,1024]{2,1,0:T(2,128)(2,1)S(1)} async-done(((bf16[512,2,1024]{2,1,0:T(2,128)(2,1)}), bf16[512,2,1024]{2,1,0:T(2,128)(2,1)S(1)}, u32[]{:S(2)}, u32[]{:S(2)}) %all-to-all-start) | async-done | bytes 2097184 | tf_op jit(solution)/shard_map/all_to_all | solution.py:202
  102.1 1.9 copy.17
  104.0 5.5 %gram.1 = (f32[128,8,128]{2,1,0:T(8,128)}, f32[128,8,128]{2,1,0:T(8,128)}) custom-call(s32[1]{0:T(128)} %bitcast.core_ref, s32[4,128]{1,0:T(4,128)} %fusion.1.slot_ref, f32[4,128]{1,0:T(4,128)} %datum_ref.1, f32[4,128]{1,0:T(4,128)} %spread_ref.1, bf16[64,2,8,1024]{3,2,1,0:T(8,128)(2,1)} %bitcast.12), custom_call_target="tpu_custom_call" | custom-call | tf_op jit(solution)/shard_map/gram/pallas_call | solution.py:210
  109.5 1.7 collective-permute-start
  111.2 1.7 collective-permute-done
  113.0 1.1 add.27
  114.1 31.0 %all_to_all.20 = f32[128,8,128]{2,1,0:T(8,128)S(1)} all-to-all(f32[128,8,128]{2,1,0:T(8,128)S(1)} %add.27), channel_id=1, replica_groups=mesh['mem_0'=4,'mem_1'=4,'mem_2'=2,'cell'=8] {'mem_0','mem_1','cell'}, dimensions={0} | all-to-all | bytes 1048576 | tf_op jit(solution)/shard_map/all_to_all | solution.py:220
  145.1 0.1 reduce_sum.9
  145.3 24.8 %all_to_all.21.own_ref = f32[128,8,128]{2,1,0:T(8,128)S(1)} all-to-all(f32[128,8,128]{2,1,0:T(8,128)S(1)} %broadcast_in_dim.2), channel_id=1, replica_groups=mesh['mem_0'=4,'mem_1'=4,'mem_2'=2,'cell'=8] {'mem_0','mem_1','cell'}, dimensions={0} | all-to-all | bytes 1048576 | tf_op jit(solution)/shard_map/all_to_all | solution.py:222
  170.1 0.0 copy-start
  170.1 2.9 collective-permute-start.1
  173.0 3.8 %mean.1 = (bf16[64,2,8,1024]{3,2,1,0:T(8,128)(2,1)}, f32[2,1024]{1,0:T(2,128)}) custom-call(bf16[64,2,8,1024]{3,2,1,0:T(8,128)(2,1)} %bitcast.13), custom_call_target="tpu_custom_call" | custom-call | tf_op jit(solution)/shard_map/mean/pallas_call | solution.py:224
  176.7 0.0 collective-permute-done.1.other_ref
  176.7 0.0 copy-start.1
  176.7 0.0 copy-done
  176.8 0.8 copy-done.1
  177.6 24.0 %analysis.1 = bf16[64,2,8,1024]{3,2,1,0:T(8,128)(2,1)} custom-call(s32[1]{0:T(128)} %bitcast.core_ref, f32[128,8,128]{2,1,0:T(8,128)} %copy-done, f32[128,8,128]{2,1,0:T(8,128)} %copy-done.1, bf16[64,2,8,1024]{3,2,1,0:T(8,128)(2,1)} %get-tuple-element.11.anomalies_ref, f32[2,1024]{1,0:T(2,128)} %get-tuple-element.12.mean_ref), custom_call_target="tpu_custom_call" | custom-call | tf_op jit(solution)/shard_map/analysis/pallas_call | solution.py:233
  201.5 1.8 copy_bitcast_fusion.1
  203.3 2.2 copy.12
  205.4 31.9 %all_to_all.22 = bf16[512,2,1024]{2,1,0:T(2,128)(2,1)} all-to-all(bf16[512,2,1024]{2,1,0:T(2,128)(2,1)S(1)} %copy.12), channel_id=1, replica_groups=mesh['mem_0'=4,'mem_1'=4,'mem_2'=2,'cell'=8] {'mem_0','mem_1','mem_2'}, dimensions={0} | all-to-all | bytes 4194304 | tf_op jit(solution)/shard_map/all_to_all | solution.py:242
  237.4 64.9 %unpack.1 = bf16[16,2,32768]{2,1,0:T(2,128)(2,1)} custom-call(bf16[32,16,2,1024]{3,2,1,0:T(2,128)(2,1)} %bitcast.16), custom_call_target="tpu_custom_call" | custom-call | tf_op jit(solution)/shard_map/unpack/pallas_call | solution.py:243
  (1 shorter events, 0.0 us)
Async XLA Ops:
  64.9 8.6 %copy-start.2 = (s32[4,128]{1,0:T(4,128)S(1)}, s32[4,128]{1,0:T(4,128)}, u32[]{:S(2)}) copy-start(s32[4,128]{1,0:T(4,128)} %param.5) | copy-start | bytes 6148
  64.9 37.2 %all-to-all-start = ((bf16[512,2,1024]{2,1,0:T(2,128)(2,1)}), bf16[512,2,1024]{2,1,0:T(2,128)(2,1)S(1)}, u32[]{:S(2)}, u32[]{:S(2)}) async-start(bf16[512,2,1024]{2,1,0:T(2,128)(2,1)} %bitcast.15), calls=%async_computation | async-start | bytes 4194304 | tf_op jit(solution)/shard_map/all_to_all | solution.py:202
  109.5 3.5 %collective-permute-start = (f32[128,8,128]{2,1,0:T(8,128)}, f32[128,8,128]{2,1,0:T(8,128)S(1)}, u32[]{:S(2)}, u32[]{:S(2)}) collective-permute-start(f32[128,8,128]{2,1,0:T(8,128)} %get-tuple-element.10), channel_id=1, source_target_pairs={{0,8},{8,0},{1,9},{9,1},{2,10},{10,2},{3,11},{11,3},{4,12},{12,4},... | collective-permute-start | bytes 1572872 | tf_op jit(solution)/shard_map/ppermute | solution.py:219
  170.1 6.7 %copy-start = (f32[128,8,128]{2,1,0:T(8,128)}, f32[128,8,128]{2,1,0:T(8,128)S(1)}, u32[]{:S(2)}) copy-start(f32[128,8,128]{2,1,0:T(8,128)S(1)} %all_to_all.21.own_ref) | copy-start | bytes 1572868
  170.1 6.7 %collective-permute-start.1 = (f32[128,8,128]{2,1,0:T(8,128)S(1)}, f32[128,8,128]{2,1,0:T(8,128)S(1)}, u32[]{:S(2)}, u32[]{:S(2)}) collective-permute-start(f32[128,8,128]{2,1,0:T(8,128)S(1)} %all_to_all.21.own_ref), channel_id=1, source_target_pairs={{0,8},{8,0},{1,9},{9,1},{2,10},{10,2},{3,11},{11,3},{4,12},{12,4},... | collective-permute-start | bytes 1572872 | tf_op jit(solution)/shard_map/ppermute | solution.py:223
  176.7 0.8 copy-start.1

commit v2 on v1

v2 whole, which is shorter than its diff:
```python
import math

import jax
import jax.numpy as jnp
from jax import lax
from jax.experimental import pallas as pl
from jax.experimental.pallas import tpu as pltpu
from jax.sharding import Mesh
from jax.sharding import PartitionSpec as P

NS_ITERS = 8
MEM = ("mem_0", "mem_1", "mem_2")
PLANE = ("mem_0", "mem_1")
F32 = jnp.float32
BF16 = jnp.bfloat16
VMEM = pl.BlockSpec(memory_space=pltpu.VMEM)
SMEM = pl.BlockSpec(memory_space=pltpu.SMEM)


def tiles_of(members):
    blocks = members // 128
    return [
        (row * 128 + i * 8, column * 128)
        for row in range(blocks)
        for column in range(row, blocks)
        for i in range(16)
    ]


def rows_of(x_ref, f):
    groups, _, rows, width = x_ref.shape
    return x_ref[:, f].reshape(groups * rows, width)


def contract(a, b, dims):
    return lax.dot_general(a, b, (dims, ((), ())), preferred_element_type=F32)


def gram_kernel(core_ref, slot_ref, datum_ref, spread_ref, x_ref, keep_ref, send_ref, sum_ref):
    groups, fields, rows, width = x_ref.shape
    members = groups * rows
    norm_factor = math.sqrt(members - 1)
    scaled_parts, innovation_parts = [], []
    iota = lax.broadcasted_iota(jnp.int32, (width, 256), 0)

    def pair(ref, r):
        return jnp.concatenate([ref[r : r + 1, :], ref[r + 1 : r + 2, :]], axis=1)

    for r in range(0, slot_ref.shape[0], 2):
        slot = pair(slot_ref, r)
        picked = None
        for f in range(fields):
            chosen = jnp.where(iota == slot - f * width, 1.0, 0.0).astype(BF16)
            term = contract(rows_of(x_ref, f), chosen, ((1,), (0,)))
            picked = term if picked is None else picked + term
        mean = jnp.sum(picked, axis=0, keepdims=True) / members
        anomaly = (picked - mean).astype(BF16).astype(F32)
        error = pair(spread_ref, r)
        scaled_parts.append((anomaly / (error * norm_factor)).astype(BF16))
        innovation_parts.append(((pair(datum_ref, r) - mean) / error).astype(BF16))
    scaled = jnp.concatenate(scaled_parts, axis=1)
    innovation = jnp.concatenate(innovation_parts, axis=1).astype(F32)
    innovation = jnp.broadcast_to(innovation, (16, innovation.shape[1])).astype(BF16)
    gram = contract(scaled, scaled, ((1,), (1,)))
    projected = contract(innovation, scaled, ((1,), (1,)))
    tiles = tiles_of(members)
    for t, (row, column) in enumerate(tiles):
        sum_ref[t] = gram[row : row + 8, column : column + 128]
    sum_ref[len(tiles) :] = jnp.zeros_like(sum_ref[len(tiles) :])
    for j in range(members // 128):
        sum_ref[len(tiles), j : j + 1, :] = projected[0:1, j * 128 : (j + 1) * 128]
    core = core_ref[0]
    half = keep_ref.shape[0]
    keep_ref[...] = sum_ref[pl.ds(core * half, half)]
    send_ref[...] = sum_ref[pl.ds((1 - core) * half, half)]


def mean_kernel(x_ref, anomalies_ref, mean_ref):
    groups, fields, rows, width = x_ref.shape
    members = groups * rows
    for f in range(fields):
        x = x_ref[:, f].astype(F32)
        mean = jnp.sum(jnp.sum(x, axis=0), axis=0, keepdims=True) / members
        mean_ref[f : f + 1, :] = mean
        anomalies_ref[:, f] = (x - mean[None]).astype(BF16)


def halves(a):
    high = a.astype(BF16)
    return high, (a - high.astype(F32)).astype(BF16)


def thirds(row):
    high = row.astype(BF16).astype(F32)
    rest = row - high
    middle = rest.astype(BF16).astype(F32)
    low = rest - middle
    pad = jnp.zeros((13, row.shape[1]), F32)
    return jnp.concatenate([high, middle, low, pad], axis=0).astype(BF16)


def times(a, b):
    dims = ((1,), (0,))
    return contract(a[0], b[0], dims) + (contract(a[0], b[1], dims) + contract(a[1], b[0], dims))


def analysis_kernel(
    core_ref, own_ref, other_ref, anomalies_ref, mean_ref, o_ref, sum_ref, sys_ref, yh, yl, zh, zl, zf
):
    members = sys_ref.shape[0]
    norm_factor = math.sqrt(members - 1)
    blocks = members // 128
    core = core_ref[0]
    half = own_ref.shape[0]
    sum_ref[pl.ds(core * half, half)] = own_ref[...]
    sum_ref[pl.ds((1 - core) * half, half)] = other_ref[...]
    tiles = tiles_of(members)
    for t, (row, column) in enumerate(tiles):
        sys_ref[row : row + 8, column : column + 128] = sum_ref[t]
    for i in range(blocks):
        for j in range(i + 1, blocks):
            upper = sys_ref[i * 128 : i * 128 + 128, j * 128 : j * 128 + 128]
            sys_ref[j * 128 : j * 128 + 128, i * 128 : i * 128 + 128] = jnp.transpose(upper)
    projected = jnp.concatenate([sum_ref[len(tiles), j : j + 1, :] for j in range(blocks)], axis=1)
    row_iota = lax.broadcasted_iota(jnp.int32, (members, members), 0)
    column_iota = lax.broadcasted_iota(jnp.int32, (members, members), 1)
    diagonal = row_iota == column_iota
    system = sys_ref[...] + jnp.where(diagonal, 1.0, 0.0)
    squares = jnp.sum(jnp.sum(system * system, axis=0, keepdims=True), axis=1, keepdims=True)
    norm_scale = jnp.sqrt(squares)
    start_y = system / norm_scale

    def step_of(product):
        return jnp.where(diagonal, 1.5, 0.0) - 0.5 * product

    first = step_of(start_y)
    first_parts = halves(first)
    zh[...], zl[...] = first_parts
    yh[...], yl[...] = halves(times(first_parts, halves(start_y)))

    def turn(_, carry):
        y, z = (yh[...], yl[...]), (zh[...], zl[...])
        step = halves(step_of(times(z, y)))
        yh[...], yl[...] = halves(times(step, y))
        zh[...], zl[...] = halves(times(step, z))
        return carry

    lax.fori_loop(0, NS_ITERS - 2, turn, 0)
    z = (zh[...], zl[...])
    step = halves(step_of(times(z, (yh[...], yl[...]))))
    zf[...] = times(step, z)
    iterate_z = zf[...]
    root = jnp.sqrt(norm_scale)
    dims = ((1,), (0,))
    z = halves(iterate_z)
    three = thirds(projected)
    sent = contract(three, z[0], dims) + contract(three, z[1], dims)
    shift = jnp.sum(sent, axis=0, keepdims=True) / (root * norm_factor)
    weights = (iterate_z / root).astype(BF16)
    combined = jnp.sum(contract(thirds(shift), weights, dims), axis=0, keepdims=True)
    combined = thirds(combined)
    groups, fields, rows, width = anomalies_ref.shape
    for f in range(fields):
        anomalies = rows_of(anomalies_ref, f)
        mean_shift = jnp.sum(contract(combined, anomalies, dims), axis=0, keepdims=True)
        base = mean_ref[f : f + 1, :] + mean_shift
        updated = contract(weights, anomalies, dims)
        o_ref[:, f] = (base + updated).astype(BF16).reshape(groups, rows, width)


def shape(dims, dtype):
    return jax.ShapeDtypeStruct(dims, dtype)


def total_for(part, sources, targets):
    total = jnp.sum(part.reshape(sources, -1, *part.shape[1:]), axis=0)
    copies = jnp.broadcast_to(total[None], (targets, *total.shape))
    return copies.reshape(-1, *total.shape[1:])


def local(prior_ensemble, measurement_location, measurement_datum, measurement_spread):
    rows, fields, span = prior_ensemble.shape
    peers = lax.axis_size(MEM)
    members = rows * peers
    width = span // peers
    core = lax.axis_index("mem_2").reshape(1).astype(jnp.int32)
    state = prior_ensemble.reshape(rows, fields, peers, width).transpose(2, 1, 0, 3)
    state = lax.all_to_all(state, MEM, 0, 0, tiled=True)
    sites = span * lax.axis_size("cell")
    block_start = (lax.axis_index("cell") * peers + lax.axis_index(MEM)) * width
    slots = measurement_location // sites * width + (measurement_location % sites - block_start)
    plane, planes = lax.axis_size(PLANE), lax.axis_size("cell")
    share = -(-(len(tiles_of(members)) + 1) // (2 * plane))
    half = shape((share * plane, 8, 128), F32)
    both = pltpu.VMEM((2 * share * plane, 8, 128), F32)
    keep, send = pl.pallas_call(
        gram_kernel,
        out_shape=(half, half),
        in_specs=[SMEM, VMEM, VMEM, VMEM, VMEM],
        out_specs=(VMEM, VMEM),
        scratch_shapes=[both],
        name="gram",
    )(core, slots, measurement_datum, measurement_spread, state)
    swap = [(0, 1), (1, 0)]
    part = keep + lax.ppermute(send, "mem_2", swap)
    part = lax.all_to_all(part, PLANE, 0, 0, tiled=True)
    part = total_for(part, plane, planes)
    part = lax.all_to_all(part, "cell", 0, 0, tiled=True)
    part = total_for(part, planes, plane)
    own = lax.all_to_all(part, PLANE, 0, 0, tiled=True)
    other = lax.ppermute(own, "mem_2", swap)
    anomalies, mean = pl.pallas_call(
        mean_kernel,
        out_shape=(shape(state.shape, BF16), shape((fields, width), F32)),
        in_specs=[VMEM],
        out_specs=(VMEM, VMEM),
        name="mean",
    )(state)
    square = pltpu.VMEM((members, members), BF16)
    whole = pltpu.VMEM((members, members), F32)
    analysis = pl.pallas_call(
        analysis_kernel,
        out_shape=shape(state.shape, BF16),
        in_specs=[SMEM, VMEM, VMEM, VMEM, VMEM],
        out_specs=VMEM,
        scratch_shapes=[both, whole, square, square, square, square, whole],
        name="analysis",
    )(core, own, other, anomalies, mean)
    returned = lax.all_to_all(analysis, MEM, 0, 0, tiled=True)
    return returned.transpose(2, 1, 0, 3).reshape(rows, fields, span)


def solution(mesh):
    torus = Mesh(
        mesh.devices.reshape(4, 4, 2, mesh.shape["cell"]), ("mem_0", "mem_1", "mem_2", "cell")
    )
    in_specs = (P(MEM, None, "cell"), P("cell", MEM), P("cell", MEM), P("cell", MEM))
    out_specs = P(MEM, None, "cell")
    return jax.shard_map(local, mesh=torus, in_specs=in_specs, out_specs=out_specs, check_vma=False)
```

time: 303 us -> 163 us (0.54)
  Pallas kernels: 163 us -> 32.3 us
  blocking collectives: 87.7 us -> 72.5 us
  local copies, waits for them, and re-layouts: 6.7 us -> 11.8 us
    pallas_call x3 -> x1, Pallas kernels: 135 us -> 4.47 us  [local(): pl.pallas_call(gram_kernel, out_shape=(half, half), in_specs=[SMEM, VMEM,...]
    all_to_all x2 -> x3, blocking collectives: 55.8 us -> 40.3 us  [the longest x1 16.7 us: local(): part = lax.all_to_all(part, 'cell', 0, 0, tiled=True)]
    reshape x3 -> x4, local copies, waits for them, and re-layouts: 5.85 us -> 9.68 us  [the longest x2 5.77 us: local(): prior_ensemble.reshape(rows, fields, peers, width).transpose(2, 1, 0, 3)]
  transfers between devices with their start and end apart: 3 -> 3, of which waited for: 2 -> 2; matrix products, arithmetic and copies ran while one was open for 0% -> 0% of each run, Pallas kernels for 1% -> 2%
where the time goes in v2:
time: 163 us; the launch traced here: 162 us
  blocking collectives  72.5 us (44%)
  Pallas kernels  32.3 us (20%)
  waiting for transfers between devices  29.5 us (18%)
  starting transfers between devices  14.5 us (9%)
  local copies, waits for them, and re-layouts  11.8 us (7%)
  other arithmetic  1.69 us (1%)
    all_to_all x1, blocking collectives, local(): returned = lax.all_to_all(analysis, MEM, 0, 0, tiled=True)  32.2 us
    all_to_all x1, waiting for transfers between devices, local(): state = lax.all_to_all(state, MEM, 0, 0, tiled=True)  28 us
    pallas_call x1, Pallas kernels, local(): pl.pallas_call(analysis_kernel, out_shape=shape(state.shape, BF16), in_sp...  24.1 us
    all_to_all x1, blocking collectives, local(): part = lax.all_to_all(part, 'cell', 0, 0, tiled=True)  16.7 us
    all_to_all x1, blocking collectives, local(): part = lax.all_to_all(part, PLANE, 0, 0, tiled=True)  12.2 us
    all_to_all x1, blocking collectives, local(): own = lax.all_to_all(part, PLANE, 0, 0, tiled=True)  11.4 us
    all_to_all x1, starting transfers between devices, local(): state = lax.all_to_all(state, MEM, 0, 0, tiled=True)  8.71 us
    reshape x2, local copies, waits for them, and re-layouts, local(): prior_ensemble.reshape(rows, fields, peers, width).transpose(2, 1, 0, 3)  5.77 us
  transfers between devices with their start and end apart: 3, of which 2 were waited for; matrix products, arithmetic and copies ran while one was open for 0% of the time, Pallas kernels for 2%

profile of v2, /device:TPU:1, one launch (start us, length us, event | category | flops | bytes accessed | tf_op | source)
XLA Modules:
  0.0 162.4 jit_solution(6584086259120829899)
XLA Ops:
  0.0 3.3 %reshape.30 = bf16[16,2,32,1024]{3,2,1,0:T(8,128)(2,1)S(1)} reshape(bf16[16,2,32768]{2,1,0:T(2,128)(2,1)} %param.4) | data formatting | bytes 4194304 | tf_op jit(solution)/shard_map/reshape | solution.py:187
  3.3 2.5 %copy.18 = bf16[16,2,32,1024]{3,0,1,2:T(8,128)(2,1)} copy(bf16[16,2,32,1024]{3,2,1,0:T(8,128)(2,1)S(1)} %reshape.30) | data formatting | bytes 4194304 | tf_op jit(solution)/shard_map/reshape | solution.py:187
  5.8 0.0 copy-start.3
  5.8 8.7 %all-to-all-start = ((bf16[32,2,16,1024]{3,2,1,0:T(8,128)(2,1)}), bf16[32,2,16,1024]{3,2,1,0:T(8,128)(2,1)S(1)}, u32[]{:S(2)}, u32[]{:S(2)}) async-start(bf16[32,2,16,1024]{3,2,1,0:T(8,128)(2,1)} %bitcast.11), calls=%async_computation | async-start | bytes 4194304 | tf_op jit(solution)/shard_map/all_to_all | solution.py:188
  14.5 0.0 copy-done.3
  14.5 0.6 fusion.1.slot_ref
  15.1 28.0 %all-to-all-done.x_ref = bf16[32,2,16,1024]{3,2,1,0:T(8,128)(2,1)S(1)} async-done(((bf16[32,2,16,1024]{3,2,1,0:T(8,128)(2,1)}), bf16[32,2,16,1024]{3,2,1,0:T(8,128)(2,1)S(1)}, u32[]{:S(2)}, u32[]{:S(2)}) %all-to-all-start) | async-done | bytes 2097184 | tf_op jit(solution)/shard_map/all_to_all | solution.py:188
  43.1 0.0 copy-start
  43.1 1.3 copy-done
  44.4 4.5 %gram.1 = (f32[96,8,128]{2,1,0:T(8,128)}, f32[96,8,128]{2,1,0:T(8,128)}) custom-call(s32[1]{0:T(128)} %bitcast.core_ref, s32[4,128]{1,0:T(4,128)} %fusion.1.slot_ref, f32[4,128]{1,0:T(4,128)} %datum_ref.1, f32[4,128]{1,0:T(4,128)} %spread_ref.1, bf16[32,2,16,1024]{3,2,1,0:T(8,128)(2,1)} %copy-done), custom_call_target="tpu_custom_call" | custom-call | tf_op jit(solution)/shard_map/gram/pallas_call | solution.py:196
  48.9 1.7 %collective-permute-start = (f32[96,8,128]{2,1,0:T(8,128)}, f32[96,8,128]{2,1,0:T(8,128)S(1)}, u32[]{:S(2)}, u32[]{:S(2)}) collective-permute-start(f32[96,8,128]{2,1,0:T(8,128)} %get-tuple-element.10), channel_id=1, source_target_pairs={{0,8},{8,0},{1,9},{9,1},{2,10},{10,2},{3,11},{11,3},{4,12},{12,4},... | collective-permute-start | bytes 1179656 | tf_op jit(solution)/shard_map/ppermute | solution.py:205
  50.6 1.6 collective-permute-done
  52.1 1.1 add.27
  53.2 12.2 %all_to_all.25 = f32[96,8,128]{2,1,0:T(8,128)S(1)} all-to-all(f32[96,8,128]{2,1,0:T(8,128)S(1)} %add.27), channel_id=1, replica_groups=mesh['mem_0'=4,'mem_1'=4,'mem_2'=2,'cell'=8] {'mem_0','mem_1'}, dimensions={0} | all-to-all | bytes 786432 | tf_op jit(solution)/shard_map/all_to_all | solution.py:206
  65.5 16.7 %all_to_all.26 = f32[48,8,128]{2,1,0:T(8,128)S(1)} all-to-all(f32[48,8,128]{2,1,0:T(8,128)S(1)} %bitcast.16), channel_id=1, replica_groups=mesh['mem_0'=4,'mem_1'=4,'mem_2'=2,'cell'=8] {'cell'}, dimensions={0} | all-to-all | bytes 393216 | tf_op jit(solution)/shard_map/all_to_all | solution.py:208
  82.2 11.4 %all_to_all.27.own_ref = f32[96,8,128]{2,1,0:T(8,128)S(1)} all-to-all(f32[96,8,128]{2,1,0:T(8,128)S(1)} %bitcast.14), channel_id=1, replica_groups=mesh['mem_0'=4,'mem_1'=4,'mem_2'=2,'cell'=8] {'mem_0','mem_1'}, dimensions={0} | all-to-all | bytes 786432 | tf_op jit(solution)/shard_map/all_to_all | solution.py:210
  93.7 0.0 copy-start.1
  93.7 4.1 %collective-permute-start.1 = (f32[96,8,128]{2,1,0:T(8,128)S(1)}, f32[96,8,128]{2,1,0:T(8,128)S(1)}, u32[]{:S(2)}, u32[]{:S(2)}) collective-permute-start(f32[96,8,128]{2,1,0:T(8,128)S(1)} %all_to_all.27.own_ref), channel_id=1, source_target_pairs={{0,8},{8,0},{1,9},{9,1},{2,10},{10,2},{3,11},{11,3},{4,12},{12,4},... | collective-permute-start | bytes 1179656 | tf_op jit(solution)/shard_map/ppermute | solution.py:211
  97.8 3.7 %mean.1 = (bf16[32,2,16,1024]{3,2,1,0:T(8,128)(2,1)}, f32[2,1024]{1,0:T(2,128)}) custom-call(bf16[32,2,16,1024]{3,2,1,0:T(8,128)(2,1)} %copy-done), custom_call_target="tpu_custom_call" | custom-call | tf_op jit(solution)/shard_map/mean/pallas_call | solution.py:212
  101.5 0.0 collective-permute-done.1.other_ref
  101.5 0.0 copy-start.2
  101.5 0.0 copy-done.1
  101.5 0.7 copy-done.2
  102.3 24.1 %analysis.1 = bf16[32,2,16,1024]{3,2,1,0:T(8,128)(2,1)} custom-call(s32[1]{0:T(128)} %bitcast.core_ref, f32[96,8,128]{2,1,0:T(8,128)} %copy-done.1, f32[96,8,128]{2,1,0:T(8,128)} %copy-done.2, bf16[32,2,16,1024]{3,2,1,0:T(8,128)(2,1)} %get-tuple-element.11.anomalies_ref, f32[2,1024]{1,0:T(2,128)} %get-tuple-element.12.mean_ref), custom_call_target="tpu_custom_call" | custom-call | tf_op jit(solution)/shard_map/analysis/pallas_call | solution.py:221
  126.3 32.2 %all_to_all.28 = bf16[32,2,16,1024]{3,2,1,0:T(8,128)(2,1)S(1)} all-to-all(bf16[32,2,16,1024]{3,2,1,0:T(8,128)(2,1)} %analysis.1), channel_id=1, replica_groups=mesh['mem_0'=4,'mem_1'=4,'mem_2'=2,'cell'=8] {'mem_0','mem_1','mem_2'}, dimensions={0} | all-to-all | bytes 4194304 | tf_op jit(solution)/shard_map/all_to_all | solution.py:229
  158.5 1.2 copy.15
  159.7 2.8 %reshape.31 = bf16[16,2,32768]{2,1,0:T(2,128)(2,1)} reshape(bf16[16,2,32,1024]{3,2,1,0:T(8,128)(2,1)S(1)} %copy.15) | data formatting | bytes 4194304 | tf_op jit(solution)/shard_map/reshape | solution.py:230
  (4 shorter events, 0.1 us)
Async XLA Ops:
  5.8 8.7 %copy-start.3 = (s32[4,128]{1,0:T(4,128)S(1)}, s32[4,128]{1,0:T(4,128)}, u32[]{:S(2)}) copy-start(s32[4,128]{1,0:T(4,128)} %param.5) | copy-start | bytes 6148
  5.8 37.3 %all-to-all-start = ((bf16[32,2,16,1024]{3,2,1,0:T(8,128)(2,1)}), bf16[32,2,16,1024]{3,2,1,0:T(8,128)(2,1)S(1)}, u32[]{:S(2)}, u32[]{:S(2)}) async-start(bf16[32,2,16,1024]{3,2,1,0:T(8,128)(2,1)} %bitcast.11), calls=%async_computation | async-start | bytes 4194304 | tf_op jit(solution)/shard_map/all_to_all | solution.py:188
  43.1 1.3 copy-start
  48.9 3.3 %collective-permute-start = (f32[96,8,128]{2,1,0:T(8,128)}, f32[96,8,128]{2,1,0:T(8,128)S(1)}, u32[]{:S(2)}, u32[]{:S(2)}) collective-permute-start(f32[96,8,128]{2,1,0:T(8,128)} %get-tuple-element.10), channel_id=1, source_target_pairs={{0,8},{8,0},{1,9},{9,1},{2,10},{10,2},{3,11},{11,3},{4,12},{12,4},... | collective-permute-start | bytes 1179656 | tf_op jit(solution)/shard_map/ppermute | solution.py:205
  93.7 7.9 %copy-start.1 = (f32[96,8,128]{2,1,0:T(8,128)}, f32[96,8,128]{2,1,0:T(8,128)S(1)}, u32[]{:S(2)}) copy-start(f32[96,8,128]{2,1,0:T(8,128)S(1)} %all_to_all.27.own_ref) | copy-start | bytes 1179652
  93.7 7.9 %collective-permute-start.1 = (f32[96,8,128]{2,1,0:T(8,128)S(1)}, f32[96,8,128]{2,1,0:T(8,128)S(1)}, u32[]{:S(2)}, u32[]{:S(2)}) collective-permute-start(f32[96,8,128]{2,1,0:T(8,128)S(1)} %all_to_all.27.own_ref), channel_id=1, source_target_pairs={{0,8},{8,0},{1,9},{9,1},{2,10},{10,2},{3,11},{11,3},{4,12},{12,4},... | collective-permute-start | bytes 1179656 | tf_op jit(solution)/shard_map/ppermute | solution.py:211
  101.5 0.7 copy-start.2

commit v3 on v2

--- a/solution.py
+++ b/solution.py
@@ -14,7 +14,52 @@
 F32 = jnp.float32
 BF16 = jnp.bfloat16
 VMEM = pl.BlockSpec(memory_space=pltpu.VMEM)
+HBM = pl.BlockSpec(memory_space=pltpu.HBM)
 SMEM = pl.BlockSpec(memory_space=pltpu.SMEM)
+
+
+def pack_kernel(x_ref, o_ref, buffer, sem, packed, sent):
+    parts, width = buffer.shape[0], o_ref.shape[3]
+    span = buffer.shape[3]
+    each = span // width
+    copies = [
+        pltpu.make_async_copy(x_ref.at[:, :, pl.ds(i * span, span)], buffer.at[i], sem.at[i])
+        for i in range(parts)
+    ]
+    for c in copies:
+        c.start()
+    results = [
+        pltpu.make_async_copy(
+            packed.at[pl.ds(i * each, each)], o_ref.at[pl.ds(i * each, each)], sent.at[i]
+        )
+        for i in range(parts)
+    ]
+    for i in range(parts):
+        copies[i].wait()
+        for k in range(each):
+            block = buffer[i, :, :, k * width : (k + 1) * width]
+            packed[i * each + k] = jnp.transpose(block, (1, 0, 2))
+        results[i].start()
+    for c in results:
+        c.wait()
+
+
+def unpack_kernel(y_ref, o_ref, buffer, sem):
+    parts, width = buffer.shape[0], y_ref.shape[3]
+    span = buffer.shape[3]
+    each = span // width
+    copies = []
+    for i in range(parts):
+        for k in range(each):
+            block = jnp.transpose(y_ref[i * each + k], (1, 0, 2))
+            buffer[i, :, :, k * width : (k + 1) * width] = block
+        copy = pltpu.make_async_copy(
+            buffer.at[i], o_ref.at[:, :, pl.ds(i * span, span)], sem.at[i]
+        )
+        copy.start()
+        copies.append(copy)
+    for c in copies:
+        c.wait()
 
 
 def tiles_of(members):
@@ -99,14 +144,50 @@
     return jnp.concatenate([high, middle, low, pad], axis=0).astype(BF16)
 
 
-def times(a, b):
+def product(a, b):
+    size = a[0].shape[0]
+    half = size // 2
     dims = ((1,), (0,))
-    return contract(a[0], b[0], dims) + (contract(a[0], b[1], dims) + contract(a[1], b[0], dims))
+
+    def block(r, c):
+        ah, al = (m[r : r + half, :] for m in a)
+        bh, bl = (m[:, c : c + half] for m in b)
+        return contract(ah, bh, dims) + (contract(ah, bl, dims) + contract(al, bh, dims))
+
+    return block(0, 0), block(0, half), block(half, half)
+
+
+def keep_product(pair, blocks):
+    high_ref, low_ref = pair
+    half = high_ref.shape[0] // 2
+    first, side, last = blocks
+    places = ((0, 0, first), (0, half, side), (half, half, last), (half, 0, jnp.transpose(side)))
+    for r, c, value in places:
+        high, low = halves(value)
+        high_ref[r : r + half, c : c + half] = high
+        low_ref[r : r + half, c : c + half] = low
 
 
 def analysis_kernel(
-    core_ref, own_ref, other_ref, anomalies_ref, mean_ref, o_ref, sum_ref, sys_ref, yh, yl, zh, zl, zf
+    core_ref,
+    own_ref,
+    other_ref,
+    source_ref,
+    mean_ref,
+    o_ref,
+    anomalies_ref,
+    sem,
+    sum_ref,
+    sys_ref,
+    yh,
+    yl,
+    zh,
+    zl,
+    th,
+    tl,
 ):
+    load = pltpu.make_async_copy(source_ref, anomalies_ref, sem)
+    load.start()
     members = sys_ref.shape[0]
     norm_factor = math.sqrt(members - 1)
     blocks = members // 128
@@ -130,36 +211,45 @@
     norm_scale = jnp.sqrt(squares)
     start_y = system / norm_scale
 
-    def step_of(product):
-        return jnp.where(diagonal, 1.5, 0.0) - 0.5 * product
-
-    first = step_of(start_y)
-    first_parts = halves(first)
-    zh[...], zl[...] = first_parts
-    yh[...], yl[...] = halves(times(first_parts, halves(start_y)))
+    half_size = members // 2
+    half_diagonal = diagonal[:half_size, :half_size]
+    y, z, t = (yh, yl), (zh, zl), (th, tl)
+
+    def step_of(blocks):
+        first, side, last = blocks
+        whole = jnp.where(half_diagonal, 1.5, 0.0)
+        return whole - 0.5 * first, -0.5 * side, whole - 0.5 * last
+
+    zh[...], zl[...] = halves(jnp.where(diagonal, 1.5, 0.0) - 0.5 * start_y)
+    th[...], tl[...] = halves(start_y)
+    keep_product(y, product(z, t))
 
     def turn(_, carry):
-        y, z = (yh[...], yl[...]), (zh[...], zl[...])
-        step = halves(step_of(times(z, y)))
-        yh[...], yl[...] = halves(times(step, y))
-        zh[...], zl[...] = halves(times(step, z))
+        keep_product(t, step_of(product(z, y)))
+        next_y, next_z = product(t, y), product(t, z)
+        keep_product(y, next_y)
+        keep_product(z, next_z)
         return carry
 
     lax.fori_loop(0, NS_ITERS - 2, turn, 0)
-    z = (zh[...], zl[...])
-    step = halves(step_of(times(z, (yh[...], yl[...]))))
-    zf[...] = times(step, z)
-    iterate_z = zf[...]
+    keep_product(t, step_of(product(z, y)))
+    first, side, last = product(t, z)
+    sys_ref[:half_size, :half_size] = first
+    sys_ref[:half_size, half_size:] = side
+    sys_ref[half_size:, half_size:] = last
+    sys_ref[half_size:, :half_size] = jnp.transpose(side)
+    iterate_z = sys_ref[...]
     root = jnp.sqrt(norm_scale)
     dims = ((1,), (0,))
-    z = halves(iterate_z)
+    zs = halves(iterate_z)
     three = thirds(projected)
-    sent = contract(three, z[0], dims) + contract(three, z[1], dims)
+    sent = contract(three, zs[0], dims) + contract(three, zs[1], dims)
     shift = jnp.sum(sent, axis=0, keepdims=True) / (root * norm_factor)
     weights = (iterate_z / root).astype(BF16)
     combined = jnp.sum(contract(thirds(shift), weights, dims), axis=0, keepdims=True)
     combined = thirds(combined)
     groups, fields, rows, width = anomalies_ref.shape
+    load.wait()
     for f in range(fields):
         anomalies = rows_of(anomalies_ref, f)
         mean_shift = jnp.sum(contract(combined, anomalies, dims), axis=0, keepdims=True)
@@ -168,8 +258,12 @@
         o_ref[:, f] = (base + updated).astype(BF16).reshape(groups, rows, width)
 
 
-def shape(dims, dtype):
-    return jax.ShapeDtypeStruct(dims, dtype)
+def far(a):
+    return pltpu.with_memory_space_constraint(a, pltpu.HBM)
+
+
+def near(a):
+    return pltpu.with_memory_space_constraint(a, pltpu.VMEM)
 
 
 def total_for(part, sources, targets):
@@ -184,14 +278,25 @@
     members = rows * peers
     width = span // peers
     core = lax.axis_index("mem_2").reshape(1).astype(jnp.int32)
-    state = prior_ensemble.reshape(rows, fields, peers, width).transpose(2, 1, 0, 3)
-    state = lax.all_to_all(state, MEM, 0, 0, tiled=True)
+    parts = 4
+    staging = [pltpu.VMEM((parts, rows, fields, span // parts), BF16), pltpu.SemaphoreType.DMA((parts,))]
+    tiled = pltpu.VMEM((peers, fields, rows, width), BF16)
+    packed = pl.pallas_call(
+        pack_kernel,
+        out_shape=pltpu.HBM(tiled.shape, BF16),
+        in_specs=[HBM],
+        out_specs=HBM,
+        scratch_shapes=staging + [tiled, pltpu.SemaphoreType.DMA((parts,))],
+        compiler_params=pltpu.CompilerParams(vmem_limit_bytes=8 << 20),
+        name="pack",
+    )(far(prior_ensemble))
+    state = near(lax.all_to_all(packed, MEM, 0, 0, tiled=True))
     sites = span * lax.axis_size("cell")
     block_start = (lax.axis_index("cell") * peers + lax.axis_index(MEM)) * width
     slots = measurement_location // sites * width + (measurement_location % sites - block_start)
     plane, planes = lax.axis_size(PLANE), lax.axis_size("cell")
     share = -(-(len(tiles_of(members)) + 1) // (2 * plane))
-    half = shape((share * plane, 8, 128), F32)
+    half = pltpu.VMEM((share * plane, 8, 128), F32)
     both = pltpu.VMEM((2 * share * plane, 8, 128), F32)
     keep, send = pl.pallas_call(
         gram_kernel,
@@ -199,6 +304,7 @@
         in_specs=[SMEM, VMEM, VMEM, VMEM, VMEM],
         out_specs=(VMEM, VMEM),
         scratch_shapes=[both],
+        compiler_params=pltpu.CompilerParams(vmem_limit_bytes=24 << 20),
         name="gram",
     )(core, slots, measurement_datum, measurement_spread, state)
     swap = [(0, 1), (1, 0)]
@@ -206,28 +312,39 @@
     part = lax.all_to_all(part, PLANE, 0, 0, tiled=True)
     part = total_for(part, plane, planes)
     part = lax.all_to_all(part, "cell", 0, 0, tiled=True)
+    anomalies, mean = pl.pallas_call(
+        mean_kernel,
+        out_shape=(pltpu.HBM(tiled.shape, BF16), pltpu.VMEM((fields, width), F32)),
+        in_specs=[VMEM],
+        out_specs=(VMEM, VMEM),
+        compiler_params=pltpu.CompilerParams(vmem_limit_bytes=24 << 20),
+        name="mean",
+    )(state)
+    part, anomalies, mean = lax.optimization_barrier((part, anomalies, mean))
     part = total_for(part, planes, plane)
     own = lax.all_to_all(part, PLANE, 0, 0, tiled=True)
     other = lax.ppermute(own, "mem_2", swap)
-    anomalies, mean = pl.pallas_call(
-        mean_kernel,
-        out_shape=(shape(state.shape, BF16), shape((fields, width), F32)),
-        in_specs=[VMEM],
-        out_specs=(VMEM, VMEM),
-        name="mean",
-    )(state)
     square = pltpu.VMEM((members, members), BF16)
     whole = pltpu.VMEM((members, members), F32)
     analysis = pl.pallas_call(
         analysis_kernel,
-        out_shape=shape(state.shape, BF16),
-        in_specs=[SMEM, VMEM, VMEM, VMEM, VMEM],
+        out_shape=tiled,
+        in_specs=[SMEM, VMEM, VMEM, HBM, VMEM],
         out_specs=VMEM,
-        scratch_shapes=[both, whole, square, square, square, square, whole],
+        scratch_shapes=[tiled, pltpu.SemaphoreType.DMA, both, whole] + [square] * 6,
+        compiler_params=pltpu.CompilerParams(vmem_limit_bytes=32 << 20),
         name="analysis",
-    )(core, own, other, anomalies, mean)
+    )(core, near(own), near(other), far(anomalies), near(mean))
     returned = lax.all_to_all(analysis, MEM, 0, 0, tiled=True)
-    return returned.transpose(2, 1, 0, 3).reshape(rows, fields, span)
+    return pl.pallas_call(
+        unpack_kernel,
+        out_shape=jax.ShapeDtypeStruct(prior_ensemble.shape, BF16),
+        in_specs=[VMEM],
+        out_specs=HBM,
+        scratch_shapes=staging,
+        compiler_params=pltpu.CompilerParams(vmem_limit_bytes=8 << 20),
+        name="unpack",
+    )(near(returned))
 
 
 def solution(mesh):

time: 163 us -> 143 us (0.88)
  blocking collectives: 72.5 us -> 55.2 us
  local copies, waits for them, and re-layouts: 11.8 us -> 0.73 us
  starting transfers between devices: 14.5 us -> 22.8 us
  waiting for transfers between devices: 29.5 us -> 37.8 us
  Pallas kernels: 32.3 us -> 25.6 us
    all_to_all x1 -> x0, blocking collectives: 16.7 us -> none  [local(): part = lax.all_to_all(part, 'cell', 0, 0, tiled=True)]
    reshape x4 -> x0, local copies, waits for them, and re-layouts: 9.68 us -> none  [the longest x2 5.77 us: local(): prior_ensemble.reshape(rows, fields, peers, width).transpose(2, 1, 0, 3)]
    all_to_all x1 -> x2, starting transfers between devices: 8.71 us -> 16.9 us  [the longest x1 8.72 us: local(): state = near(lax.all_to_all(packed, MEM, 0, 0, tiled=True))]
    all_to_all x1 -> x2, waiting for transfers between devices: 28 us -> 35.1 us  [the longest x1 28.5 us: local(): state = near(lax.all_to_all(packed, MEM, 0, 0, tiled=True))]
    pallas_call x2 -> x4, Pallas kernels: 27.8 us -> 23.6 us  [the longest x1 17.5 us: local(): pl.pallas_call(analysis_kernel, out_shape=tiled, in_specs=[SMEM, VMEM, VM...]
    pallas_call x1, Pallas kernels: 4.47 us -> 1.97 us  [local(): pl.pallas_call(gram_kernel, out_shape=(half, half), in_specs=[SMEM, VMEM,...]
    unnamed x8 -> x6, local copies, waits for them, and re-layouts: 2.06 us -> 0.02 us
  transfers between devices with their start and end apart: 3 -> 4, of which waited for: 2 -> 4; matrix products, arithmetic and copies ran while one was open for 0% -> 0% of each run, Pallas kernels for 2% -> 1%
where the time goes in v3:
time: 143 us; the launch traced here: 142 us
  blocking collectives  55.2 us (39%)
  waiting for transfers between devices  37.8 us (26%)
  Pallas kernels  25.6 us (18%)
  starting transfers between devices  22.8 us (16%)
    all_to_all x1, blocking collectives, local(): returned = lax.all_to_all(analysis, MEM, 0, 0, tiled=True)  31.6 us
    all_to_all x1, waiting for transfers between devices, local(): state = near(lax.all_to_all(packed, MEM, 0, 0, tiled=True))  28.5 us
    pallas_call x1, Pallas kernels, local(): pl.pallas_call(analysis_kernel, out_shape=tiled, in_specs=[SMEM, VMEM, VM...  17.5 us
    all_to_all x1, blocking collectives, local(): part = lax.all_to_all(part, PLANE, 0, 0, tiled=True)  12.2 us
    all_to_all x1, blocking collectives, local(): own = lax.all_to_all(part, PLANE, 0, 0, tiled=True)  11.4 us
    all_to_all x1, starting transfers between devices, local(): state = near(lax.all_to_all(packed, MEM, 0, 0, tiled=True))  8.72 us
    all_to_all x1, starting transfers between devices, local(): part = lax.all_to_all(part, 'cell', 0, 0, tiled=True)  8.19 us
    all_to_all x1, waiting for transfers between devices, local(): part = lax.all_to_all(part, 'cell', 0, 0, tiled=True)  6.6 us
  transfers between devices with their start and end apart: 4, of which 4 were waited for; matrix products, arithmetic and copies ran while one was open for 0% of the time, Pallas kernels for 1%

profile of v3, /device:TPU:1, one launch (start us, length us, event | category | flops | bytes accessed | tf_op | source)
XLA Modules:
  0.0 142.5 jit_solution(17318688762911157747)
XLA Ops:
  0.0 2.5 %pack.1 = bf16[32,2,16,1024]{3,2,1,0:T(8,128)(2,1)} custom-call(bf16[16,2,32768]{2,1,0:T(2,128)(2,1)} %x_ref.1), custom_call_target="tpu_custom_call" | custom-call | tf_op jit(solution)/shard_map/pack/pallas_call | solution.py:284
  2.5 0.0 copy-start.2
  2.5 0.0 copy-start
  2.6 0.0 copy-start.1
  2.6 8.7 %all-to-all-start = ((bf16[32,2,16,1024]{3,2,1,0:T(8,128)(2,1)}), bf16[32,2,16,1024]{3,2,1,0:T(8,128)(2,1)S(1)}, u32[]{:S(2)}, u32[]{:S(2)}) async-start(bf16[32,2,16,1024]{3,2,1,0:T(8,128)(2,1)} %pack.1), calls=%async_computation | async-start | bytes 4194304 | tf_op jit(solution)/shard_map/all_to_all | solution.py:293
  11.3 0.0 copy-done.2
  11.3 28.5 %all-to-all-done.x_ref = bf16[32,2,16,1024]{3,2,1,0:T(8,128)(2,1)S(1)} async-done(((bf16[32,2,16,1024]{3,2,1,0:T(8,128)(2,1)}), bf16[32,2,16,1024]{3,2,1,0:T(8,128)(2,1)S(1)}, u32[]{:S(2)}, u32[]{:S(2)}) %all-to-all-start) | async-done | bytes 2097184 | tf_op jit(solution)/shard_map/all_to_all | solution.py:293
  39.9 0.0 copy-done
  39.9 0.0 copy-done.1
  39.9 2.0 %gram.1 = (f32[96,8,128]{2,1,0:T(8,128)S(1)}, f32[96,8,128]{2,1,0:T(8,128)S(1)}) custom-call(s32[1]{0:T(128)} %bitcast.core_ref, s32[4,128]{1,0:T(4,128)S(1)} %fusion.1.slot_ref, f32[4,128]{1,0:T(4,128)S(1)} %copy-done, f32[4,128]{1,0:T(4,128)S(1)} %copy-done.1, bf16[32,2,16,1024]{3,2,1,0:T(8,128)(2,1)S(1)} %all-to-all-done.x_ref), custom_call_target="tpu_custom_call" | custom-call | tf_op jit(solution)/shard_map/gram/pallas_call | solution.py:301
  41.9 1.8 %collective-permute-start = (f32[96,8,128]{2,1,0:T(8,128)S(1)}, f32[96,8,128]{2,1,0:T(8,128)S(1)}, u32[]{:S(2)}, u32[]{:S(2)}) collective-permute-start(f32[96,8,128]{2,1,0:T(8,128)S(1)} %get-tuple-element.13), channel_id=1, source_target_pairs={{0,8},{8,0},{1,9},{9,1},{2,10},{10,2},{3,11},{11,3},{4,12},{12,4},... | collective-permute-start | bytes 1179656 | tf_op jit(solution)/shard_map/ppermute | solution.py:311
  43.7 1.3 collective-permute-done
  45.0 0.1 add.27
  45.1 12.2 %all_to_all.25 = f32[96,8,128]{2,1,0:T(8,128)S(1)} all-to-all(f32[96,8,128]{2,1,0:T(8,128)S(1)} %add.27), channel_id=1, replica_groups=mesh['mem_0'=4,'mem_1'=4,'mem_2'=2,'cell'=8] {'mem_0','mem_1'}, dimensions={0} | all-to-all | bytes 786432 | tf_op jit(solution)/shard_map/all_to_all | solution.py:312
  57.3 0.7 broadcast_in_dim.4
  58.0 8.2 %all-to-all-start.2 = ((f32[48,8,128]{2,1,0:T(8,128)}), f32[48,8,128]{2,1,0:T(8,128)S(1)}, u32[]{:S(2)}, u32[]{:S(2)}) async-start(f32[48,8,128]{2,1,0:T(8,128)} %bitcast.2), calls=%async_computation.2 | async-start | bytes 393216 | tf_op jit(solution)/shard_map/all_to_all | solution.py:314
  66.2 2.1 %mean.1 = (bf16[32,2,16,1024]{3,2,1,0:T(8,128)(2,1)}, f32[2,1024]{1,0:T(2,128)S(1)}) custom-call(bf16[32,2,16,1024]{3,2,1,0:T(8,128)(2,1)S(1)} %all-to-all-done.x_ref), custom_call_target="tpu_custom_call" | custom-call | tf_op jit(solution)/shard_map/mean/pallas_call | solution.py:315
  68.3 6.6 %all-to-all-done.2 = f32[48,8,128]{2,1,0:T(8,128)S(1)} async-done(((f32[48,8,128]{2,1,0:T(8,128)}), f32[48,8,128]{2,1,0:T(8,128)S(1)}, u32[]{:S(2)}, u32[]{:S(2)}) %all-to-all-start.2) | async-done | bytes 196640 | tf_op jit(solution)/shard_map/all_to_all | solution.py:314
  75.0 11.4 %all_to_all.26.own_ref = f32[96,8,128]{2,1,0:T(8,128)S(1)} all-to-all(f32[96,8,128]{2,1,0:T(8,128)S(1)} %bitcast.6), channel_id=1, replica_groups=mesh['mem_0'=4,'mem_1'=4,'mem_2'=2,'cell'=8] {'mem_0','mem_1'}, dimensions={0} | all-to-all | bytes 786432 | tf_op jit(solution)/shard_map/all_to_all | solution.py:325
  86.4 4.1 %collective-permute-start.1 = (f32[96,8,128]{2,1,0:T(8,128)S(1)}, f32[96,8,128]{2,1,0:T(8,128)S(1)}, u32[]{:S(2)}, u32[]{:S(2)}) collective-permute-start(f32[96,8,128]{2,1,0:T(8,128)S(1)} %all_to_all.26.own_ref), channel_id=1, source_target_pairs={{0,8},{8,0},{1,9},{9,1},{2,10},{10,2},{3,11},{11,3},{4,12},{12,4},... | collective-permute-start | bytes 1179656 | tf_op jit(solution)/shard_map/ppermute | solution.py:326
  90.5 1.3 collective-permute-done.1.other_ref
  91.9 17.5 %analysis.1 = bf16[32,2,16,1024]{3,2,1,0:T(8,128)(2,1)S(1)} custom-call(s32[1]{0:T(128)} %bitcast.core_ref, f32[96,8,128]{2,1,0:T(8,128)S(1)} %all_to_all.26.own_ref, f32[96,8,128]{2,1,0:T(8,128)S(1)} %collective-permute-done.1.other_ref, bf16[32,2,16,1024]{3,2,1,0:T(8,128)(2,1)} %get-tuple-element.17.source_ref, f32[2,1024]{1,0:T(2,128)S(1)} %get-tuple-element.18.mean_ref), custom_call_target="tpu_custom_call" | custom-call | tf_op jit(solution)/shard_map/analysis/pallas_call | solution.py:329
  109.4 31.6 %all_to_all.27.y_ref = bf16[32,2,16,1024]{3,2,1,0:T(8,128)(2,1)S(1)} all-to-all(bf16[32,2,16,1024]{3,2,1,0:T(8,128)(2,1)S(1)} %analysis.1), channel_id=1, replica_groups=mesh['mem_0'=4,'mem_1'=4,'mem_2'=2,'cell'=8] {'mem_0','mem_1','mem_2'}, dimensions={0} | all-to-all | bytes 4194304 | tf_op jit(solution)/shard_map/all_to_all | solution.py:338
  141.0 1.4 %unpack.1 = bf16[16,2,32768]{2,1,0:T(2,128)(2,1)} custom-call(bf16[32,2,16,1024]{3,2,1,0:T(8,128)(2,1)S(1)} %all_to_all.27.y_ref), custom_call_target="tpu_custom_call" | custom-call | tf_op jit(solution)/shard_map/unpack/pallas_call | solution.py:339
  (4 shorter events, 0.1 us)
Async XLA Ops:
  2.5 8.8 %copy-start.2 = (s32[4,128]{1,0:T(4,128)S(1)}, s32[4,128]{1,0:T(4,128)}, u32[]{:S(2)}) copy-start(s32[4,128]{1,0:T(4,128)} %param.5) | copy-start | bytes 6148
  2.5 37.3 %copy-start = (f32[4,128]{1,0:T(4,128)S(1)}, f32[4,128]{1,0:T(4,128)}, u32[]{:S(2)}) copy-start(f32[4,128]{1,0:T(4,128)} %datum_ref.1) | copy-start | bytes 6148
  2.6 37.3 %copy-start.1 = (f32[4,128]{1,0:T(4,128)S(1)}, f32[4,128]{1,0:T(4,128)}, u32[]{:S(2)}) copy-start(f32[4,128]{1,0:T(4,128)} %spread_ref.1) | copy-start | bytes 6148
  2.6 37.3 %all-to-all-start = ((bf16[32,2,16,1024]{3,2,1,0:T(8,128)(2,1)}), bf16[32,2,16,1024]{3,2,1,0:T(8,128)(2,1)S(1)}, u32[]{:S(2)}, u32[]{:S(2)}) async-start(bf16[32,2,16,1024]{3,2,1,0:T(8,128)(2,1)} %pack.1), calls=%async_computation | async-start | bytes 4194304 | tf_op jit(solution)/shard_map/all_to_all | solution.py:293
  41.9 3.1 %collective-permute-start = (f32[96,8,128]{2,1,0:T(8,128)S(1)}, f32[96,8,128]{2,1,0:T(8,128)S(1)}, u32[]{:S(2)}, u32[]{:S(2)}) collective-permute-start(f32[96,8,128]{2,1,0:T(8,128)S(1)} %get-tuple-element.13), channel_id=1, source_target_pairs={{0,8},{8,0},{1,9},{9,1},{2,10},{10,2},{3,11},{11,3},{4,12},{12,4},... | collective-permute-start | bytes 1179656 | tf_op jit(solution)/shard_map/ppermute | solution.py:311
  58.0 16.9 %all-to-all-start.2 = ((f32[48,8,128]{2,1,0:T(8,128)}), f32[48,8,128]{2,1,0:T(8,128)S(1)}, u32[]{:S(2)}, u32[]{:S(2)}) async-start(f32[48,8,128]{2,1,0:T(8,128)} %bitcast.2), calls=%async_computation.2 | async-start | bytes 393216 | tf_op jit(solution)/shard_map/all_to_all | solution.py:314
  86.4 5.5 %collective-permute-start.1 = (f32[96,8,128]{2,1,0:T(8,128)S(1)}, f32[96,8,128]{2,1,0:T(8,128)S(1)}, u32[]{:S(2)}, u32[]{:S(2)}) collective-permute-start(f32[96,8,128]{2,1,0:T(8,128)S(1)} %all_to_all.26.own_ref), channel_id=1, source_target_pairs={{0,8},{8,0},{1,9},{9,1},{2,10},{10,2},{3,11},{11,3},{4,12},{12,4},... | collective-permute-start | bytes 1179656 | tf_op jit(solution)/shard_map/ppermute | solution.py:326

commit v4 on v3

--- a/solution.py
+++ b/solution.py
@@ -1,3 +1,4 @@
+import functools
 import math
 
 import jax
@@ -81,7 +82,9 @@
     return lax.dot_general(a, b, (dims, ((), ())), preferred_element_type=F32)
 
 
-def gram_kernel(core_ref, slot_ref, datum_ref, spread_ref, x_ref, keep_ref, send_ref, sum_ref):
+def gram_kernel(
+    core_ref, start_ref, location_ref, datum_ref, spread_ref, x_ref, keep_ref, send_ref, sum_ref, *, sites
+):
     groups, fields, rows, width = x_ref.shape
     members = groups * rows
     norm_factor = math.sqrt(members - 1)
@@ -91,11 +94,12 @@
     def pair(ref, r):
         return jnp.concatenate([ref[r : r + 1, :], ref[r + 1 : r + 2, :]], axis=1)
 
-    for r in range(0, slot_ref.shape[0], 2):
-        slot = pair(slot_ref, r)
+    start = start_ref[0]
+    for r in range(0, location_ref.shape[0], 2):
+        location = pair(location_ref, r)
         picked = None
         for f in range(fields):
-            chosen = jnp.where(iota == slot - f * width, 1.0, 0.0).astype(BF16)
+            chosen = jnp.where(iota == location - (start + f * sites), 1.0, 0.0).astype(BF16)
             term = contract(rows_of(x_ref, f), chosen, ((1,), (0,)))
             picked = term if picked is None else picked + term
         mean = jnp.sum(picked, axis=0, keepdims=True) / members
@@ -111,9 +115,12 @@
     tiles = tiles_of(members)
     for t, (row, column) in enumerate(tiles):
         sum_ref[t] = gram[row : row + 8, column : column + 128]
-    sum_ref[len(tiles) :] = jnp.zeros_like(sum_ref[len(tiles) :])
-    for j in range(members // 128):
-        sum_ref[len(tiles), j : j + 1, :] = projected[0:1, j * 128 : (j + 1) * 128]
+    rows = jnp.concatenate(
+        [projected[0:1, j * 128 : (j + 1) * 128] for j in range(members // 128)], axis=0
+    )
+    rows = jnp.concatenate([rows, pltpu.roll(rows, 64, 1)], axis=0)
+    low_lanes = lax.broadcasted_iota(jnp.int32, rows.shape, 1) < 64
+    sum_ref[len(tiles) - 1] = jnp.where(low_lanes, rows, sum_ref[len(tiles) - 1])
     core = core_ref[0]
     half = keep_ref.shape[0]
     keep_ref[...] = sum_ref[pl.ds(core * half, half)]
@@ -202,7 +209,13 @@
         for j in range(i + 1, blocks):
             upper = sys_ref[i * 128 : i * 128 + 128, j * 128 : j * 128 + 128]
             sys_ref[j * 128 : j * 128 + 128, i * 128 : i * 128 + 128] = jnp.transpose(upper)
-    projected = jnp.concatenate([sum_ref[len(tiles), j : j + 1, :] for j in range(blocks)], axis=1)
+    tile = sum_ref[len(tiles) - 1]
+    low_lanes = lax.broadcasted_iota(jnp.int32, (blocks, 128), 1) < 64
+    projected = jnp.where(low_lanes, tile[0:blocks], pltpu.roll(tile[blocks : 2 * blocks], 64, 1))
+    projected = jnp.concatenate([projected[j : j + 1, :] for j in range(blocks)], axis=1)
+    corner = sys_ref[members - 128 :, members - 128 :]
+    low_lanes = lax.broadcasted_iota(jnp.int32, tile.shape, 1) < 64
+    sys_ref[members - 8 :, members - 128 :] = jnp.where(low_lanes, jnp.transpose(corner)[120:128], tile)
     row_iota = lax.broadcasted_iota(jnp.int32, (members, members), 0)
     column_iota = lax.broadcasted_iota(jnp.int32, (members, members), 1)
     diagonal = row_iota == column_iota
@@ -266,10 +279,17 @@
     return pltpu.with_memory_space_constraint(a, pltpu.VMEM)
 
 
-def total_for(part, sources, targets):
-    total = jnp.sum(part.reshape(sources, -1, *part.shape[1:]), axis=0)
-    copies = jnp.broadcast_to(total[None], (targets, *total.shape))
-    return copies.reshape(-1, *total.shape[1:])
+def total_along(part, axis):
+    size = lax.axis_size(axis)
+    assert size == 8
+
+    def moved(a, shift):
+        return lax.ppermute(a, axis, [(i, (i + shift) % size) for i in range(size)])
+
+    before, after = moved(part, 1), moved(part, -1)
+    two = before + part
+    three = two + after
+    return three + (moved(three, 3) + moved(two, -3))
 
 
 def local(prior_ensemble, measurement_location, measurement_datum, measurement_spread):
@@ -290,28 +310,28 @@
         compiler_params=pltpu.CompilerParams(vmem_limit_bytes=8 << 20),
         name="pack",
     )(far(prior_ensemble))
-    state = near(lax.all_to_all(packed, MEM, 0, 0, tiled=True))
     sites = span * lax.axis_size("cell")
     block_start = (lax.axis_index("cell") * peers + lax.axis_index(MEM)) * width
-    slots = measurement_location // sites * width + (measurement_location % sites - block_start)
-    plane, planes = lax.axis_size(PLANE), lax.axis_size("cell")
-    share = -(-(len(tiles_of(members)) + 1) // (2 * plane))
+    block_start = block_start.reshape(1).astype(jnp.int32)
+    packed, core, block_start = lax.optimization_barrier((packed, core, block_start))
+    state = near(lax.all_to_all(packed, MEM, 0, 0, tiled=True))
+    plane = lax.axis_size(PLANE)
+    share = -(-len(tiles_of(members)) // (2 * plane))
     half = pltpu.VMEM((share * plane, 8, 128), F32)
     both = pltpu.VMEM((2 * share * plane, 8, 128), F32)
     keep, send = pl.pallas_call(
-        gram_kernel,
+        functools.partial(gram_kernel, sites=sites),
         out_shape=(half, half),
-        in_specs=[SMEM, VMEM, VMEM, VMEM, VMEM],
+        in_specs=[SMEM, SMEM, VMEM, VMEM, VMEM, VMEM],
         out_specs=(VMEM, VMEM),
         scratch_shapes=[both],
         compiler_params=pltpu.CompilerParams(vmem_limit_bytes=24 << 20),
         name="gram",
-    )(core, slots, measurement_datum, measurement_spread, state)
+    )(core, block_start, measurement_location, measurement_datum, measurement_spread, state)
     swap = [(0, 1), (1, 0)]
     part = keep + lax.ppermute(send, "mem_2", swap)
     part = lax.all_to_all(part, PLANE, 0, 0, tiled=True)
-    part = total_for(part, plane, planes)
-    part = lax.all_to_all(part, "cell", 0, 0, tiled=True)
+    part = jnp.sum(part.reshape(plane, share, 8, 128), axis=0)
     anomalies, mean = pl.pallas_call(
         mean_kernel,
         out_shape=(pltpu.HBM(tiled.shape, BF16), pltpu.VMEM((fields, width), F32)),
@@ -321,7 +341,8 @@
         name="mean",
     )(state)
     part, anomalies, mean = lax.optimization_barrier((part, anomalies, mean))
-    part = total_for(part, planes, plane)
+    part = total_along(part, "cell")
+    part = jnp.broadcast_to(part[None], (plane, *part.shape)).reshape(half.shape)
     own = lax.all_to_all(part, PLANE, 0, 0, tiled=True)
     other = lax.ppermute(own, "mem_2", swap)
     square = pltpu.VMEM((members, members), BF16)

time: 143 us -> 141 us (0.986)
  blocking collectives: 55.2 us -> 79.3 us
  waiting for transfers between devices: 37.8 us -> 14.6 us
  starting transfers between devices: 22.8 us -> 19.6 us
    all_to_all x2 -> x1, waiting for transfers between devices: 35.1 us -> 6.85 us  [local(): part = lax.all_to_all(part, PLANE, 0, 0, tiled=True)]
    all_to_all x1, blocking collectives: 12.2 us -> 37 us  [local(): state = near(lax.all_to_all(packed, MEM, 0, 0, tiled=True))]
    all_to_all x2 -> x1, starting transfers between devices: 16.9 us -> 3.54 us  [local(): part = lax.all_to_all(part, PLANE, 0, 0, tiled=True)]
    ppermute x0 -> x4, starting transfers between devices: none -> 10.3 us  [moved(): return lax.ppermute(a, axis, [(i, (i + shift) % size) for i in range(size)])]
    ppermute x0 -> x4, waiting for transfers between devices: none -> 5.26 us  [moved(): return lax.ppermute(a, axis, [(i, (i + shift) % size) for i in range(size)])]
  transfers between devices with their start and end apart: 4 -> 7, of which waited for: 4 -> 6; matrix products, arithmetic and copies ran while one was open for 0% -> 0% of each run, Pallas kernels for 1% -> 2%
where the time goes in v4:
time: 141 us; the launch traced here: 140 us
  blocking collectives  79.3 us (56%)
  Pallas kernels  25.7 us (18%)
  starting transfers between devices  19.6 us (14%)
  waiting for transfers between devices  14.6 us (10%)
    all_to_all x1, blocking collectives, local(): state = near(lax.all_to_all(packed, MEM, 0, 0, tiled=True))  37 us
    all_to_all x1, blocking collectives, local(): returned = lax.all_to_all(analysis, MEM, 0, 0, tiled=True)  31.6 us
    pallas_call x1, Pallas kernels, local(): pl.pallas_call(analysis_kernel, out_shape=tiled, in_specs=[SMEM, VMEM, VM...  17.5 us
    all_to_all x1, blocking collectives, local(): own = lax.all_to_all(part, PLANE, 0, 0, tiled=True)  10.8 us
    ppermute x4, starting transfers between devices, moved(): return lax.ppermute(a, axis, [(i, (i + shift) % size) for i in range(size)])  10.3 us
    all_to_all x1, waiting for transfers between devices, local(): part = lax.all_to_all(part, PLANE, 0, 0, tiled=True)  6.85 us
    ppermute x1, starting transfers between devices, local(): other = lax.ppermute(own, 'mem_2', swap)  5.3 us
    ppermute x4, waiting for transfers between devices, moved(): return lax.ppermute(a, axis, [(i, (i + shift) % size) for i in range(size)])  5.26 us
  transfers between devices with their start and end apart: 7, of which 6 were waited for; matrix products, arithmetic and copies ran while one was open for 0% of the time, Pallas kernels for 2%

profile of v4, /device:TPU:1, one launch (start us, length us, event | category | flops | bytes accessed | tf_op | source)
XLA Modules:
  0.0 140.3 jit_solution(14882057284967179071)
XLA Ops:
  0.0 2.5 %pack.1 = bf16[32,2,16,1024]{3,2,1,0:T(8,128)(2,1)} custom-call(bf16[16,2,32768]{2,1,0:T(2,128)(2,1)} %x_ref.1), custom_call_target="tpu_custom_call" | custom-call | tf_op jit(solution)/shard_map/pack/pallas_call | solution.py:304
  2.5 0.0 copy-start
  2.6 0.0 copy-start.1
  2.6 0.0 copy-start.2
  2.6 37.0 %all_to_all.20.x_ref = bf16[32,2,16,1024]{3,2,1,0:T(8,128)(2,1)S(1)} all-to-all(bf16[32,2,16,1024]{3,2,1,0:T(8,128)(2,1)} %pack.1), channel_id=1, replica_groups=mesh['mem_0'=4,'mem_1'=4,'mem_2'=2,'cell'=8] {'mem_0','mem_1','mem_2'}, dimensions={0} | all-to-all | bytes 4194304 | tf_op jit(solution)/shard_map/all_to_all | solution.py:317
  39.6 0.0 copy-done
  39.6 0.0 copy-done.1
  39.6 0.0 copy-done.2
  39.6 2.0 %gram.1 = (f32[80,8,128]{2,1,0:T(8,128)S(1)}, f32[80,8,128]{2,1,0:T(8,128)S(1)}) custom-call(s32[1]{0:T(128)} %bitcast.core_ref, s32[1]{0:T(128)} %bitcast.1.start_ref, s32[4,128]{1,0:T(4,128)S(1)} %copy-done, f32[4,128]{1,0:T(4,128)S(1)} %copy-done.1, f32[4,128]{1,0:T(4,128)S(1)} %copy-done.2, bf16[32,2,16,1024]{3,2,1,0:T(8,128)(2,1)S(1)} %all_to_all.20.x_ref), custom_call_target="tpu_custom_call" | custom-call | tf_op jit(solution)/shard_map/gram/pallas_call | solution.py:322
  41.6 0.5 collective-permute-start
  42.1 1.3 collective-permute-done
  43.4 0.8 add.27
  44.2 3.5 %all-to-all-start.1 = ((f32[80,8,128]{2,1,0:T(8,128)}), f32[80,8,128]{2,1,0:T(8,128)S(1)}, u32[]{:S(2)}, u32[]{:S(2)}) async-start(f32[80,8,128]{2,1,0:T(8,128)} %add.27), calls=%async_computation.1 | async-start | bytes 655360 | tf_op jit(solution)/shard_map/all_to_all | solution.py:333
  47.7 2.1 %mean.1 = (bf16[32,2,16,1024]{3,2,1,0:T(8,128)(2,1)}, f32[2,1024]{1,0:T(2,128)S(1)}) custom-call(bf16[32,2,16,1024]{3,2,1,0:T(8,128)(2,1)S(1)} %all_to_all.20.x_ref), custom_call_target="tpu_custom_call" | custom-call | tf_op jit(solution)/shard_map/mean/pallas_call | solution.py:335
  49.9 6.8 %all-to-all-done.1 = f32[80,8,128]{2,1,0:T(8,128)S(1)} async-done(((f32[80,8,128]{2,1,0:T(8,128)}), f32[80,8,128]{2,1,0:T(8,128)S(1)}, u32[]{:S(2)}, u32[]{:S(2)}) %all-to-all-start.1) | async-done | bytes 327712 | tf_op jit(solution)/shard_map/all_to_all | solution.py:333
  56.7 1.7 %collective-permute-start.1 = (f32[5,8,128]{2,1,0:T(8,128)S(1)}, f32[5,8,128]{2,1,0:T(8,128)S(1)}, u32[]{:S(2)}, u32[]{:S(2)}) collective-permute-start(f32[5,8,128]{2,1,0:T(8,128)S(1)} %reduce_sum.9), channel_id=1, source_target_pairs={{0,1},{1,2},{2,3},{3,4},{4,5},{5,6},{6,7},{7,0},{8,9},{9,10},{10,1... | collective-permute-start | bytes 61448 | tf_op jit(solution)/shard_map/ppermute | solution.py:287
  58.5 4.0 %collective-permute-start.2 = (f32[5,8,128]{2,1,0:T(8,128)S(1)}, f32[5,8,128]{2,1,0:T(8,128)S(1)}, u32[]{:S(2)}, u32[]{:S(2)}) collective-permute-start(f32[5,8,128]{2,1,0:T(8,128)S(1)} %reduce_sum.9), channel_id=1, source_target_pairs={{0,7},{1,0},{2,1},{3,2},{4,3},{5,4},{6,5},{7,6},{8,15},{9,8},{10,9... | collective-permute-start | bytes 61448 | tf_op jit(solution)/shard_map/ppermute | solution.py:287
  62.5 1.1 collective-permute-done.1
  63.6 0.0 collective-permute-done.2
  63.6 4.3 %collective-permute-start.3 = (f32[5,8,128]{2,1,0:T(8,128)S(1)}, f32[5,8,128]{2,1,0:T(8,128)S(1)}, u32[]{:S(2)}, u32[]{:S(2)}) collective-permute-start(f32[5,8,128]{2,1,0:T(8,128)S(1)} %get-tuple-element.25), channel_id=1, source_target_pairs={{0,3},{1,4},{2,5},{3,6},{4,7},{5,0},{6,1},{7,2},{8,11},{9,12},{10,... | collective-permute-start | bytes 61448 | tf_op jit(solution)/shard_map/ppermute | solution.py:287
  67.9 0.3 collective-permute-start.4
  68.1 1.2 collective-permute-done.3
  69.3 3.0 %collective-permute-done.4 = f32[5,8,128]{2,1,0:T(8,128)S(1)} collective-permute-done((f32[5,8,128]{2,1,0:T(8,128)S(1)}, f32[5,8,128]{2,1,0:T(8,128)S(1)}, u32[]{:S(2)}, u32[]{:S(2)}) %collective-permute-start.4) | collective-permute-done | bytes 20512 | tf_op jit(solution)/shard_map/ppermute | solution.py:287
  72.3 10.8 %all_to_all.21.own_ref = f32[80,8,128]{2,1,0:T(8,128)S(1)} all-to-all(f32[80,8,128]{2,1,0:T(8,128)S(1)} %bitcast.5), channel_id=1, replica_groups=mesh['mem_0'=4,'mem_1'=4,'mem_2'=2,'cell'=8] {'mem_0','mem_1'}, dimensions={0} | all-to-all | bytes 655360 | tf_op jit(solution)/shard_map/all_to_all | solution.py:346
  83.1 5.3 %collective-permute-start.5 = (f32[80,8,128]{2,1,0:T(8,128)S(1)}, f32[80,8,128]{2,1,0:T(8,128)S(1)}, u32[]{:S(2)}, u32[]{:S(2)}) collective-permute-start(f32[80,8,128]{2,1,0:T(8,128)S(1)} %all_to_all.21.own_ref), channel_id=1, source_target_pairs={{0,8},{8,0},{1,9},{9,1},{2,10},{10,2},{3,11},{11,3},{4,12},{12,4},... | collective-permute-start | bytes 983048 | tf_op jit(solution)/shard_map/ppermute | solution.py:347
  88.4 1.3 collective-permute-done.5.other_ref
  89.6 17.5 %analysis.1 = bf16[32,2,16,1024]{3,2,1,0:T(8,128)(2,1)S(1)} custom-call(s32[1]{0:T(128)} %bitcast.core_ref, f32[80,8,128]{2,1,0:T(8,128)S(1)} %all_to_all.21.own_ref, f32[80,8,128]{2,1,0:T(8,128)S(1)} %collective-permute-done.5.other_ref, bf16[32,2,16,1024]{3,2,1,0:T(8,128)(2,1)} %get-tuple-element.23.source_ref, f32[2,1024]{1,0:T(2,128)S(1)} %get-tuple-element.24.mean_ref), custom_call_target="tpu_custom_call" | custom-call | tf_op jit(solution)/shard_map/analysis/pallas_call | solution.py:350
  107.2 31.6 %all_to_all.22.y_ref = bf16[32,2,16,1024]{3,2,1,0:T(8,128)(2,1)S(1)} all-to-all(bf16[32,2,16,1024]{3,2,1,0:T(8,128)(2,1)S(1)} %analysis.1), channel_id=1, replica_groups=mesh['mem_0'=4,'mem_1'=4,'mem_2'=2,'cell'=8] {'mem_0','mem_1','mem_2'}, dimensions={0} | all-to-all | bytes 4194304 | tf_op jit(solution)/shard_map/all_to_all | solution.py:359
  138.7 1.4 %unpack.1 = bf16[16,2,32768]{2,1,0:T(2,128)(2,1)} custom-call(bf16[32,2,16,1024]{3,2,1,0:T(8,128)(2,1)S(1)} %all_to_all.22.y_ref), custom_call_target="tpu_custom_call" | custom-call | tf_op jit(solution)/shard_map/unpack/pallas_call | solution.py:360
  (4 shorter events, 0.1 us)
Async XLA Ops:
  2.5 37.0 %copy-start = (s32[4,128]{1,0:T(4,128)S(1)}, s32[4,128]{1,0:T(4,128)}, u32[]{:S(2)}) copy-start(s32[4,128]{1,0:T(4,128)} %location_ref.1) | copy-start | bytes 6148
  2.6 37.0 %copy-start.1 = (f32[4,128]{1,0:T(4,128)S(1)}, f32[4,128]{1,0:T(4,128)}, u32[]{:S(2)}) copy-start(f32[4,128]{1,0:T(4,128)} %datum_ref.1) | copy-start | bytes 6148
  2.6 37.0 %copy-start.2 = (f32[4,128]{1,0:T(4,128)S(1)}, f32[4,128]{1,0:T(4,128)}, u32[]{:S(2)}) copy-start(f32[4,128]{1,0:T(4,128)} %spread_ref.1) | copy-start | bytes 6148
  41.6 1.7 %collective-permute-start = (f32[80,8,128]{2,1,0:T(8,128)S(1)}, f32[80,8,128]{2,1,0:T(8,128)S(1)}, u32[]{:S(2)}, u32[]{:S(2)}) collective-permute-start(f32[80,8,128]{2,1,0:T(8,128)S(1)} %get-tuple-element.19), channel_id=1, source_target_pairs={{0,8},{8,0},{1,9},{9,1},{2,10},{10,2},{3,11},{11,3},{4,12},{12,4},... | collective-permute-start | bytes 983048 | tf_op jit(solution)/shard_map/ppermute | solution.py:332
  44.2 12.5 %all-to-all-start.1 = ((f32[80,8,128]{2,1,0:T(8,128)}), f32[80,8,128]{2,1,0:T(8,128)S(1)}, u32[]{:S(2)}, u32[]{:S(2)}) async-start(f32[80,8,128]{2,1,0:T(8,128)} %add.27), calls=%async_computation.1 | async-start | bytes 655360 | tf_op jit(solution)/shard_map/all_to_all | solution.py:333
  56.7 6.8 %collective-permute-start.1 = (f32[5,8,128]{2,1,0:T(8,128)S(1)}, f32[5,8,128]{2,1,0:T(8,128)S(1)}, u32[]{:S(2)}, u32[]{:S(2)}) collective-permute-start(f32[5,8,128]{2,1,0:T(8,128)S(1)} %reduce_sum.9), channel_id=1, source_target_pairs={{0,1},{1,2},{2,3},{3,4},{4,5},{5,6},{6,7},{7,0},{8,9},{9,10},{10,1... | collective-permute-start | bytes 61448 | tf_op jit(solution)/shard_map/ppermute | solution.py:287
  58.5 5.1 %collective-permute-start.2 = (f32[5,8,128]{2,1,0:T(8,128)S(1)}, f32[5,8,128]{2,1,0:T(8,128)S(1)}, u32[]{:S(2)}, u32[]{:S(2)}) collective-permute-start(f32[5,8,128]{2,1,0:T(8,128)S(1)} %reduce_sum.9), channel_id=1, source_target_pairs={{0,7},{1,0},{2,1},{3,2},{4,3},{5,4},{6,5},{7,6},{8,15},{9,8},{10,9... | collective-permute-start | bytes 61448 | tf_op jit(solution)/shard_map/ppermute | solution.py:287
  63.6 5.7 %collective-permute-start.3 = (f32[5,8,128]{2,1,0:T(8,128)S(1)}, f32[5,8,128]{2,1,0:T(8,128)S(1)}, u32[]{:S(2)}, u32[]{:S(2)}) collective-permute-start(f32[5,8,128]{2,1,0:T(8,128)S(1)} %get-tuple-element.25), channel_id=1, source_target_pairs={{0,3},{1,4},{2,5},{3,6},{4,7},{5,0},{6,1},{7,2},{8,11},{9,12},{10,... | collective-permute-start | bytes 61448 | tf_op jit(solution)/shard_map/ppermute | solution.py:287
  67.9 4.4 %collective-permute-start.4 = (f32[5,8,128]{2,1,0:T(8,128)S(1)}, f32[5,8,128]{2,1,0:T(8,128)S(1)}, u32[]{:S(2)}, u32[]{:S(2)}) collective-permute-start(f32[5,8,128]{2,1,0:T(8,128)S(1)} %get-tuple-element.26), channel_id=1, source_target_pairs={{0,5},{1,6},{2,7},{3,0},{4,1},{5,2},{6,3},{7,4},{8,13},{9,14},{10,... | collective-permute-start | bytes 61448 | tf_op jit(solution)/shard_map/ppermute | solution.py:287
  83.1 6.6 %collective-permute-start.5 = (f32[80,8,128]{2,1,0:T(8,128)S(1)}, f32[80,8,128]{2,1,0:T(8,128)S(1)}, u32[]{:S(2)}, u32[]{:S(2)}) collective-permute-start(f32[80,8,128]{2,1,0:T(8,128)S(1)} %all_to_all.21.own_ref), channel_id=1, source_target_pairs={{0,8},{8,0},{1,9},{9,1},{2,10},{10,2},{3,11},{11,3},{4,12},{12,4},... | collective-permute-start | bytes 983048 | tf_op jit(solution)/shard_map/ppermute | solution.py:347

commit v5 on v4

--- a/solution.py
+++ b/solution.py
@@ -279,17 +279,12 @@
     return pltpu.with_memory_space_constraint(a, pltpu.VMEM)
 
 
-def total_along(part, axis):
-    size = lax.axis_size(axis)
-    assert size == 8
-
-    def moved(a, shift):
-        return lax.ppermute(a, axis, [(i, (i + shift) % size) for i in range(size)])
-
-    before, after = moved(part, 1), moved(part, -1)
-    two = before + part
-    three = two + after
-    return three + (moved(three, 3) + moved(two, -3))
+def spread(part, peers):
+    return jnp.broadcast_to(part[None], (peers, *part.shape)).reshape(-1, *part.shape[1:])
+
+
+def summed(part, peers):
+    return jnp.sum(part.reshape(peers, -1, *part.shape[1:]), axis=0)
 
 
 def local(prior_ensemble, measurement_location, measurement_datum, measurement_spread):
@@ -331,7 +326,9 @@
     swap = [(0, 1), (1, 0)]
     part = keep + lax.ppermute(send, "mem_2", swap)
     part = lax.all_to_all(part, PLANE, 0, 0, tiled=True)
-    part = jnp.sum(part.reshape(plane, share, 8, 128), axis=0)
+    part = summed(part, plane)
+    planes = lax.axis_size("cell")
+    part = summed(lax.all_to_all(spread(part, planes), "cell", 0, 0, tiled=True), planes)
     anomalies, mean = pl.pallas_call(
         mean_kernel,
         out_shape=(pltpu.HBM(tiled.shape, BF16), pltpu.VMEM((fields, width), F32)),
@@ -341,9 +338,7 @@
         name="mean",
     )(state)
     part, anomalies, mean = lax.optimization_barrier((part, anomalies, mean))
-    part = total_along(part, "cell")
-    part = jnp.broadcast_to(part[None], (plane, *part.shape)).reshape(half.shape)
-    own = lax.all_to_all(part, PLANE, 0, 0, tiled=True)
+    own = lax.all_to_all(spread(part, plane), PLANE, 0, 0, tiled=True)
     other = lax.ppermute(own, "mem_2", swap)
     square = pltpu.VMEM((members, members), BF16)
     whole = pltpu.VMEM((members, members), F32)

time: 141 us -> 140 us (level)
  blocking collectives: 79.3 us -> 91.4 us
  starting transfers between devices: 19.6 us -> 12.6 us
  waiting for transfers between devices: 14.6 us -> 8.76 us
    all_to_all x1 -> x2, blocking collectives: 10.8 us -> 22.8 us  [the longest x1 12.2 us: local(): part = lax.all_to_all(part, PLANE, 0, 0, tiled=True)]
    ppermute x4 -> x0, starting transfers between devices: 10.3 us -> none  [moved(): return lax.ppermute(a, axis, [(i, (i + shift) % size) for i in range(size)])]
    ppermute x4 -> x0, waiting for transfers between devices: 5.26 us -> none  [moved(): return lax.ppermute(a, axis, [(i, (i + shift) % size) for i in range(size)])]
    all_to_all x1, starting transfers between devices: 3.54 us -> 8.2 us  [local(): lax.all_to_all(spread(part, planes), 'cell', 0, 0, tiled=True)]
  transfers between devices with their start and end apart: 7 -> 3, of which waited for: 6 -> 3; matrix products, arithmetic and copies ran while one was open for 0% -> 0% of each run, Pallas kernels for 2% -> 2%
where the time goes in v5:
time: 140 us; the launch traced here: 139 us
  blocking collectives  91.4 us (65%)
  Pallas kernels  25.6 us (18%)
  starting transfers between devices  12.6 us (9%)
  waiting for transfers between devices  8.76 us (6%)
    all_to_all x1, blocking collectives, local(): state = near(lax.all_to_all(packed, MEM, 0, 0, tiled=True))  37 us
    all_to_all x1, blocking collectives, local(): returned = lax.all_to_all(analysis, MEM, 0, 0, tiled=True)  31.6 us
    pallas_call x1, Pallas kernels, local(): pl.pallas_call(analysis_kernel, out_shape=tiled, in_specs=[SMEM, VMEM, VM...  17.5 us
    all_to_all x1, blocking collectives, local(): part = lax.all_to_all(part, PLANE, 0, 0, tiled=True)  12.2 us
    all_to_all x1, blocking collectives, local(): own = lax.all_to_all(spread(part, plane), PLANE, 0, 0, tiled=True)  10.6 us
    all_to_all x1, starting transfers between devices, local(): lax.all_to_all(spread(part, planes), 'cell', 0, 0, tiled=True)  8.2 us
    all_to_all x1, waiting for transfers between devices, local(): lax.all_to_all(spread(part, planes), 'cell', 0, 0, tiled=True)  6.25 us
    ppermute x1, starting transfers between devices, local(): other = lax.ppermute(own, 'mem_2', swap)  3.9 us
  transfers between devices with their start and end apart: 3, of which 3 were waited for; matrix products, arithmetic and copies ran while one was open for 0% of the time, Pallas kernels for 2%

profile of v5, /device:TPU:1, one launch (start us, length us, event | category | flops | bytes accessed | tf_op | source)
XLA Modules:
  0.0 139.3 jit_solution(4430626142727988118)
XLA Ops:
  0.0 2.5 %pack.1 = bf16[32,2,16,1024]{3,2,1,0:T(8,128)(2,1)} custom-call(bf16[16,2,32768]{2,1,0:T(2,128)(2,1)} %x_ref.1), custom_call_target="tpu_custom_call" | custom-call | tf_op jit(solution)/shard_map/pack/pallas_call | solution.py:299
  2.5 0.0 copy-start
  2.6 0.0 copy-start.1
  2.6 0.0 copy-start.2
  2.6 37.0 %all_to_all.25.x_ref = bf16[32,2,16,1024]{3,2,1,0:T(8,128)(2,1)S(1)} all-to-all(bf16[32,2,16,1024]{3,2,1,0:T(8,128)(2,1)} %pack.1), channel_id=1, replica_groups=mesh['mem_0'=4,'mem_1'=4,'mem_2'=2,'cell'=8] {'mem_0','mem_1','mem_2'}, dimensions={0} | all-to-all | bytes 4194304 | tf_op jit(solution)/shard_map/all_to_all | solution.py:312
  39.6 0.0 copy-done
  39.6 0.0 copy-done.1
  39.6 0.0 copy-done.2
  39.6 2.0 %gram.1 = (f32[80,8,128]{2,1,0:T(8,128)S(1)}, f32[80,8,128]{2,1,0:T(8,128)S(1)}) custom-call(s32[1]{0:T(128)} %bitcast.core_ref, s32[1]{0:T(128)} %bitcast.1.start_ref, s32[4,128]{1,0:T(4,128)S(1)} %copy-done, f32[4,128]{1,0:T(4,128)S(1)} %copy-done.1, f32[4,128]{1,0:T(4,128)S(1)} %copy-done.2, bf16[32,2,16,1024]{3,2,1,0:T(8,128)(2,1)S(1)} %all_to_all.25.x_ref), custom_call_target="tpu_custom_call" | custom-call | tf_op jit(solution)/shard_map/gram/pallas_call | solution.py:317
  41.6 0.5 collective-permute-start
  42.1 1.3 collective-permute-done
  43.4 12.2 %all_to_all.26 = f32[80,8,128]{2,1,0:T(8,128)S(1)} all-to-all(f32[80,8,128]{2,1,0:T(8,128)S(1)} %add.15), channel_id=1, replica_groups=mesh['mem_0'=4,'mem_1'=4,'mem_2'=2,'cell'=8] {'mem_0','mem_1'}, dimensions={0} | all-to-all | bytes 655360 | tf_op jit(solution)/shard_map/all_to_all | solution.py:328
  55.7 0.7 broadcast_in_dim.4
  56.3 8.2 %all-to-all-start.2 = ((f32[40,8,128]{2,1,0:T(8,128)}), f32[40,8,128]{2,1,0:T(8,128)S(1)}, u32[]{:S(2)}, u32[]{:S(2)}) async-start(f32[40,8,128]{2,1,0:T(8,128)} %bitcast.3), calls=%async_computation.2 | async-start | bytes 327680 | tf_op jit(solution)/shard_map/all_to_all | solution.py:331
  64.5 2.1 %mean.1 = (bf16[32,2,16,1024]{3,2,1,0:T(8,128)(2,1)}, f32[2,1024]{1,0:T(2,128)S(1)}) custom-call(bf16[32,2,16,1024]{3,2,1,0:T(8,128)(2,1)S(1)} %all_to_all.25.x_ref), custom_call_target="tpu_custom_call" | custom-call | tf_op jit(solution)/shard_map/mean/pallas_call | solution.py:332
  66.7 6.3 %all-to-all-done.2 = f32[40,8,128]{2,1,0:T(8,128)S(1)} async-done(((f32[40,8,128]{2,1,0:T(8,128)}), f32[40,8,128]{2,1,0:T(8,128)S(1)}, u32[]{:S(2)}, u32[]{:S(2)}) %all-to-all-start.2) | async-done | bytes 163872 | tf_op jit(solution)/shard_map/all_to_all | solution.py:331
  73.0 10.6 %all_to_all.27.own_ref = f32[80,8,128]{2,1,0:T(8,128)S(1)} all-to-all(f32[80,8,128]{2,1,0:T(8,128)S(1)} %bitcast.7), channel_id=1, replica_groups=mesh['mem_0'=4,'mem_1'=4,'mem_2'=2,'cell'=8] {'mem_0','mem_1'}, dimensions={0} | all-to-all | bytes 655360 | tf_op jit(solution)/shard_map/all_to_all | solution.py:341
  83.6 3.9 %collective-permute-start.1 = (f32[80,8,128]{2,1,0:T(8,128)S(1)}, f32[80,8,128]{2,1,0:T(8,128)S(1)}, u32[]{:S(2)}, u32[]{:S(2)}) collective-permute-start(f32[80,8,128]{2,1,0:T(8,128)S(1)} %all_to_all.27.own_ref), channel_id=1, source_target_pairs={{0,8},{8,0},{1,9},{9,1},{2,10},{10,2},{3,11},{11,3},{4,12},{12,4},... | collective-permute-start | bytes 983048 | tf_op jit(solution)/shard_map/ppermute | solution.py:342
  87.5 1.3 collective-permute-done.1.other_ref
  88.7 17.5 %analysis.1 = bf16[32,2,16,1024]{3,2,1,0:T(8,128)(2,1)S(1)} custom-call(s32[1]{0:T(128)} %bitcast.core_ref, f32[80,8,128]{2,1,0:T(8,128)S(1)} %all_to_all.27.own_ref, f32[80,8,128]{2,1,0:T(8,128)S(1)} %collective-permute-done.1.other_ref, bf16[32,2,16,1024]{3,2,1,0:T(8,128)(2,1)} %get-tuple-element.23.source_ref, f32[2,1024]{1,0:T(2,128)S(1)} %get-tuple-element.24.mean_ref), custom_call_target="tpu_custom_call" | custom-call | tf_op jit(solution)/shard_map/analysis/pallas_call | solution.py:345
  106.3 31.6 %all_to_all.28.y_ref = bf16[32,2,16,1024]{3,2,1,0:T(8,128)(2,1)S(1)} all-to-all(bf16[32,2,16,1024]{3,2,1,0:T(8,128)(2,1)S(1)} %analysis.1), channel_id=1, replica_groups=mesh['mem_0'=4,'mem_1'=4,'mem_2'=2,'cell'=8] {'mem_0','mem_1','mem_2'}, dimensions={0} | all-to-all | bytes 4194304 | tf_op jit(solution)/shard_map/all_to_all | solution.py:354
  137.8 1.4 %unpack.1 = bf16[16,2,32768]{2,1,0:T(2,128)(2,1)} custom-call(bf16[32,2,16,1024]{3,2,1,0:T(8,128)(2,1)S(1)} %all_to_all.28.y_ref), custom_call_target="tpu_custom_call" | custom-call | tf_op jit(solution)/shard_map/unpack/pallas_call | solution.py:355
  (4 shorter events, 0.1 us)
Async XLA Ops:
  2.5 37.0 %copy-start = (s32[4,128]{1,0:T(4,128)S(1)}, s32[4,128]{1,0:T(4,128)}, u32[]{:S(2)}) copy-start(s32[4,128]{1,0:T(4,128)} %location_ref.1) | copy-start | bytes 6148
  2.6 37.0 %copy-start.1 = (f32[4,128]{1,0:T(4,128)S(1)}, f32[4,128]{1,0:T(4,128)}, u32[]{:S(2)}) copy-start(f32[4,128]{1,0:T(4,128)} %datum_ref.1) | copy-start | bytes 6148
  2.6 37.0 %copy-start.2 = (f32[4,128]{1,0:T(4,128)S(1)}, f32[4,128]{1,0:T(4,128)}, u32[]{:S(2)}) copy-start(f32[4,128]{1,0:T(4,128)} %spread_ref.1) | copy-start | bytes 6148
  41.6 1.7 %collective-permute-start = (f32[80,8,128]{2,1,0:T(8,128)S(1)}, f32[80,8,128]{2,1,0:T(8,128)S(1)}, u32[]{:S(2)}, u32[]{:S(2)}) collective-permute-start(f32[80,8,128]{2,1,0:T(8,128)S(1)} %get-tuple-element.19), channel_id=1, source_target_pairs={{0,8},{8,0},{1,9},{9,1},{2,10},{10,2},{3,11},{11,3},{4,12},{12,4},... | collective-permute-start | bytes 983048 | tf_op jit(solution)/shard_map/ppermute | solution.py:327
  56.3 16.6 %all-to-all-start.2 = ((f32[40,8,128]{2,1,0:T(8,128)}), f32[40,8,128]{2,1,0:T(8,128)S(1)}, u32[]{:S(2)}, u32[]{:S(2)}) async-start(f32[40,8,128]{2,1,0:T(8,128)} %bitcast.3), calls=%async_computation.2 | async-start | bytes 327680 | tf_op jit(solution)/shard_map/all_to_all | solution.py:331
  83.6 5.2 %collective-permute-start.1 = (f32[80,8,128]{2,1,0:T(8,128)S(1)}, f32[80,8,128]{2,1,0:T(8,128)S(1)}, u32[]{:S(2)}, u32[]{:S(2)}) collective-permute-start(f32[80,8,128]{2,1,0:T(8,128)S(1)} %all_to_all.27.own_ref), channel_id=1, source_target_pairs={{0,8},{8,0},{1,9},{9,1},{2,10},{10,2},{3,11},{11,3},{4,12},{12,4},... | collective-permute-start | bytes 983048 | tf_op jit(solution)/shard_map/ppermute | solution.py:342

commit v6 on v5

--- a/solution.py
+++ b/solution.py
@@ -179,11 +179,9 @@
     core_ref,
     own_ref,
     other_ref,
-    source_ref,
+    anomalies_ref,
     mean_ref,
     o_ref,
-    anomalies_ref,
-    sem,
     sum_ref,
     sys_ref,
     yh,
@@ -193,8 +191,6 @@
     th,
     tl,
 ):
-    load = pltpu.make_async_copy(source_ref, anomalies_ref, sem)
-    load.start()
     members = sys_ref.shape[0]
     norm_factor = math.sqrt(members - 1)
     blocks = members // 128
@@ -244,7 +240,7 @@
         keep_product(z, next_z)
         return carry
 
-    lax.fori_loop(0, NS_ITERS - 2, turn, 0)
+    lax.fori_loop(0, NS_ITERS - 2, turn, 0, unroll=NS_ITERS - 2)
     keep_product(t, step_of(product(z, y)))
     first, side, last = product(t, z)
     sys_ref[:half_size, :half_size] = first
@@ -262,7 +258,6 @@
     combined = jnp.sum(contract(thirds(shift), weights, dims), axis=0, keepdims=True)
     combined = thirds(combined)
     groups, fields, rows, width = anomalies_ref.shape
-    load.wait()
     for f in range(fields):
         anomalies = rows_of(anomalies_ref, f)
         mean_shift = jnp.sum(contract(combined, anomalies, dims), axis=0, keepdims=True)
@@ -331,13 +326,13 @@
     part = summed(lax.all_to_all(spread(part, planes), "cell", 0, 0, tiled=True), planes)
     anomalies, mean = pl.pallas_call(
         mean_kernel,
-        out_shape=(pltpu.HBM(tiled.shape, BF16), pltpu.VMEM((fields, width), F32)),
+        out_shape=(tiled, pltpu.VMEM((fields, width), F32)),
+        input_output_aliases={0: 0},
         in_specs=[VMEM],
         out_specs=(VMEM, VMEM),
         compiler_params=pltpu.CompilerParams(vmem_limit_bytes=24 << 20),
         name="mean",
     )(state)
-    part, anomalies, mean = lax.optimization_barrier((part, anomalies, mean))
     own = lax.all_to_all(spread(part, plane), PLANE, 0, 0, tiled=True)
     other = lax.ppermute(own, "mem_2", swap)
     square = pltpu.VMEM((members, members), BF16)
@@ -345,12 +340,12 @@
     analysis = pl.pallas_call(
         analysis_kernel,
         out_shape=tiled,
-        in_specs=[SMEM, VMEM, VMEM, HBM, VMEM],
+        in_specs=[SMEM, VMEM, VMEM, VMEM, VMEM],
         out_specs=VMEM,
-        scratch_shapes=[tiled, pltpu.SemaphoreType.DMA, both, whole] + [square] * 6,
+        scratch_shapes=[both, whole] + [square] * 6,
         compiler_params=pltpu.CompilerParams(vmem_limit_bytes=32 << 20),
         name="analysis",
-    )(core, near(own), near(other), far(anomalies), near(mean))
+    )(core, near(own), near(other), near(anomalies), near(mean))
     returned = lax.all_to_all(analysis, MEM, 0, 0, tiled=True)
     return pl.pallas_call(
         unpack_kernel,

time: 140 us -> 137 us (0.979)
  blocking collectives: 91.4 us -> 108 us
  starting transfers between devices: 12.6 us -> 4.38 us
  waiting for transfers between devices: 8.76 us -> 1.67 us
  Pallas kernels: 25.6 us -> 22.7 us
    all_to_all x0 -> x1, blocking collectives: none -> 16.4 us  [local(): lax.all_to_all(spread(part, planes), 'cell', 0, 0, tiled=True)]
    all_to_all x1 -> x0, starting transfers between devices: 8.2 us -> none  [local(): lax.all_to_all(spread(part, planes), 'cell', 0, 0, tiled=True)]
    all_to_all x1 -> x0, waiting for transfers between devices: 6.25 us -> none  [local(): lax.all_to_all(spread(part, planes), 'cell', 0, 0, tiled=True)]
    pallas_call x1, Pallas kernels: 17.5 us -> 15.9 us  [local(): pl.pallas_call(analysis_kernel, out_shape=tiled, in_specs=[SMEM, VMEM, VM...]
  transfers between devices with their start and end apart: 3 -> 2, of which waited for: 3 -> 2; matrix products, arithmetic and copies ran while one was open for 0% -> 0% of each run, Pallas kernels for 2% -> 1%
where the time goes in v6:
time: 137 us
  blocking collectives  108 us (79%)
  Pallas kernels  22.7 us (17%)
  starting transfers between devices  4.38 us (3%)
  waiting for transfers between devices  1.67 us (1%)
    all_to_all x1, blocking collectives, local(): state = near(lax.all_to_all(packed, MEM, 0, 0, tiled=True))  37 us
    all_to_all x1, blocking collectives, local(): returned = lax.all_to_all(analysis, MEM, 0, 0, tiled=True)  31.6 us
    all_to_all x1, blocking collectives, local(): lax.all_to_all(spread(part, planes), 'cell', 0, 0, tiled=True)  16.4 us
    pallas_call x1, Pallas kernels, local(): pl.pallas_call(analysis_kernel, out_shape=tiled, in_specs=[SMEM, VMEM, VM...  15.9 us
    all_to_all x1, blocking collectives, local(): part = lax.all_to_all(part, PLANE, 0, 0, tiled=True)  12.2 us
    all_to_all x1, blocking collectives, local(): own = lax.all_to_all(spread(part, plane), PLANE, 0, 0, tiled=True)  10.6 us
    ppermute x1, starting transfers between devices, local(): other = lax.ppermute(own, 'mem_2', swap)  3.9 us
  transfers between devices with their start and end apart: 2, of which 2 were waited for; matrix products, arithmetic and copies ran while one was open for 0% of the time, Pallas kernels for 1%

profile of v6, /device:TPU:1, one launch (start us, length us, event | category | flops | bytes accessed | tf_op | source)
XLA Modules:
  0.0 137.0 jit_solution(14314282436827280662)
XLA Ops:
  0.0 2.5 %pack.1 = bf16[32,2,16,1024]{3,2,1,0:T(8,128)(2,1)} custom-call(bf16[16,2,32768]{2,1,0:T(2,128)(2,1)} %x_ref.1), custom_call_target="tpu_custom_call" | custom-call | tf_op jit(solution)/shard_map/pack/pallas_call | solution.py:294
  2.5 0.0 copy-start
  2.6 0.0 copy-start.1
  2.6 0.0 copy-start.2
  2.6 37.0 %all_to_all.25.x_ref = bf16[32,2,16,1024]{3,2,1,0:T(8,128)(2,1)S(1)} all-to-all(bf16[32,2,16,1024]{3,2,1,0:T(8,128)(2,1)} %pack.1), channel_id=1, replica_groups=mesh['mem_0'=4,'mem_1'=4,'mem_2'=2,'cell'=8] {'mem_0','mem_1','mem_2'}, dimensions={0} | all-to-all | bytes 4194304 | tf_op jit(solution)/shard_map/all_to_all | solution.py:307
  39.6 0.0 copy-done
  39.6 0.0 copy-done.1
  39.6 0.0 copy-done.2
  39.6 2.0 %gram.1 = (f32[80,8,128]{2,1,0:T(8,128)S(1)}, f32[80,8,128]{2,1,0:T(8,128)S(1)}) custom-call(s32[1]{0:T(128)} %bitcast.core_ref, s32[1]{0:T(128)} %bitcast.1.start_ref, s32[4,128]{1,0:T(4,128)S(1)} %copy-done, f32[4,128]{1,0:T(4,128)S(1)} %copy-done.1, f32[4,128]{1,0:T(4,128)S(1)} %copy-done.2, bf16[32,2,16,1024]{3,2,1,0:T(8,128)(2,1)S(1)} %all_to_all.25.x_ref), custom_call_target="tpu_custom_call" | custom-call | tf_op jit(solution)/shard_map/gram/pallas_call | solution.py:312
  41.6 0.5 collective-permute-start
  42.1 1.3 collective-permute-done
  43.4 12.2 %all_to_all.26 = f32[80,8,128]{2,1,0:T(8,128)S(1)} all-to-all(f32[80,8,128]{2,1,0:T(8,128)S(1)} %add.15), channel_id=1, replica_groups=mesh['mem_0'=4,'mem_1'=4,'mem_2'=2,'cell'=8] {'mem_0','mem_1'}, dimensions={0} | all-to-all | bytes 655360 | tf_op jit(solution)/shard_map/all_to_all | solution.py:323
  55.7 16.4 %all_to_all.27 = f32[40,8,128]{2,1,0:T(8,128)S(1)} all-to-all(f32[40,8,128]{2,1,0:T(8,128)S(1)} %bitcast.9), channel_id=1, replica_groups=mesh['mem_0'=4,'mem_1'=4,'mem_2'=2,'cell'=8] {'cell'}, dimensions={0} | all-to-all | bytes 327680 | tf_op jit(solution)/shard_map/all_to_all | solution.py:326
  72.1 10.6 %all_to_all.28.own_ref = f32[80,8,128]{2,1,0:T(8,128)S(1)} all-to-all(f32[80,8,128]{2,1,0:T(8,128)S(1)} %bitcast.7), channel_id=1, replica_groups=mesh['mem_0'=4,'mem_1'=4,'mem_2'=2,'cell'=8] {'mem_0','mem_1'}, dimensions={0} | all-to-all | bytes 655360 | tf_op jit(solution)/shard_map/all_to_all | solution.py:336
  82.7 3.9 %collective-permute-start.1 = (f32[80,8,128]{2,1,0:T(8,128)S(1)}, f32[80,8,128]{2,1,0:T(8,128)S(1)}, u32[]{:S(2)}, u32[]{:S(2)}) collective-permute-start(f32[80,8,128]{2,1,0:T(8,128)S(1)} %all_to_all.28.own_ref), channel_id=1, source_target_pairs={{0,8},{8,0},{1,9},{9,1},{2,10},{10,2},{3,11},{11,3},{4,12},{12,4},... | collective-permute-start | bytes 983048 | tf_op jit(solution)/shard_map/ppermute | solution.py:337
  86.6 0.8 mean.1
  87.5 0.4 collective-permute-done.1.other_ref
  87.9 15.9 %analysis.1 = bf16[32,2,16,1024]{3,2,1,0:T(8,128)(2,1)S(1)} custom-call(s32[1]{0:T(128)} %bitcast.core_ref, f32[80,8,128]{2,1,0:T(8,128)S(1)} %all_to_all.28.own_ref, f32[80,8,128]{2,1,0:T(8,128)S(1)} %collective-permute-done.1.other_ref, bf16[32,2,16,1024]{3,2,1,0:T(8,128)(2,1)S(1)} %get-tuple-element.17.anomalies_ref, f32[2,1024]{1,0:T(2,128)S(1)} %get-tuple-element.18.mean_ref), custom_call_target="tpu_custom_call" | custom-call | tf_op jit(solution)/shard_map/analysis/pallas_call | solution.py:340
  103.8 31.6 %all_to_all.29.y_ref = bf16[32,2,16,1024]{3,2,1,0:T(8,128)(2,1)S(1)} all-to-all(bf16[32,2,16,1024]{3,2,1,0:T(8,128)(2,1)S(1)} %analysis.1), channel_id=1, replica_groups=mesh['mem_0'=4,'mem_1'=4,'mem_2'=2,'cell'=8] {'mem_0','mem_1','mem_2'}, dimensions={0} | all-to-all | bytes 4194304 | tf_op jit(solution)/shard_map/all_to_all | solution.py:349
  135.3 1.4 %unpack.1 = bf16[16,2,32768]{2,1,0:T(2,128)(2,1)} custom-call(bf16[32,2,16,1024]{3,2,1,0:T(8,128)(2,1)S(1)} %all_to_all.29.y_ref), custom_call_target="tpu_custom_call" | custom-call | tf_op jit(solution)/shard_map/unpack/pallas_call | solution.py:350
  (5 shorter events, 0.1 us)
Async XLA Ops:
  2.5 37.0 %copy-start = (s32[4,128]{1,0:T(4,128)S(1)}, s32[4,128]{1,0:T(4,128)}, u32[]{:S(2)}) copy-start(s32[4,128]{1,0:T(4,128)} %location_ref.1) | copy-start | bytes 6148
  2.6 37.0 %copy-start.1 = (f32[4,128]{1,0:T(4,128)S(1)}, f32[4,128]{1,0:T(4,128)}, u32[]{:S(2)}) copy-start(f32[4,128]{1,0:T(4,128)} %datum_ref.1) | copy-start | bytes 6148
  2.6 37.0 %copy-start.2 = (f32[4,128]{1,0:T(4,128)S(1)}, f32[4,128]{1,0:T(4,128)}, u32[]{:S(2)}) copy-start(f32[4,128]{1,0:T(4,128)} %spread_ref.1) | copy-start | bytes 6148
  41.6 1.7 %collective-permute-start = (f32[80,8,128]{2,1,0:T(8,128)S(1)}, f32[80,8,128]{2,1,0:T(8,128)S(1)}, u32[]{:S(2)}, u32[]{:S(2)}) collective-permute-start(f32[80,8,128]{2,1,0:T(8,128)S(1)} %get-tuple-element.16), channel_id=1, source_target_pairs={{0,8},{8,0},{1,9},{9,1},{2,10},{10,2},{3,11},{11,3},{4,12},{12,4},... | collective-permute-start | bytes 983048 | tf_op jit(solution)/shard_map/ppermute | solution.py:322
  82.7 5.2 %collective-permute-start.1 = (f32[80,8,128]{2,1,0:T(8,128)S(1)}, f32[80,8,128]{2,1,0:T(8,128)S(1)}, u32[]{:S(2)}, u32[]{:S(2)}) collective-permute-start(f32[80,8,128]{2,1,0:T(8,128)S(1)} %all_to_all.28.own_ref), channel_id=1, source_target_pairs={{0,8},{8,0},{1,9},{9,1},{2,10},{10,2},{3,11},{11,3},{4,12},{12,4},... | collective-permute-start | bytes 983048 | tf_op jit(solution)/shard_map/ppermute | solution.py:337

commit v7 on v6

--- a/solution.py
+++ b/solution.py
@@ -105,7 +105,7 @@
         mean = jnp.sum(picked, axis=0, keepdims=True) / members
         anomaly = (picked - mean).astype(BF16).astype(F32)
         error = pair(spread_ref, r)
-        scaled_parts.append((anomaly / (error * norm_factor)).astype(BF16))
+        scaled_parts.append((anomaly * (1.0 / (error * norm_factor))).astype(BF16))
         innovation_parts.append(((pair(datum_ref, r) - mean) / error).astype(BF16))
     scaled = jnp.concatenate(scaled_parts, axis=1)
     innovation = jnp.concatenate(innovation_parts, axis=1).astype(F32)
@@ -173,6 +173,18 @@
         high, low = halves(value)
         high_ref[r : r + half, c : c + half] = high
         low_ref[r : r + half, c : c + half] = low
+
+
+def diagonal_of(size):
+    rows = lax.broadcasted_iota(jnp.int32, (size, size), 0)
+    return rows == lax.broadcasted_iota(jnp.int32, (size, size), 1)
+
+
+def through(row, pair):
+    parts = thirds(row)
+    dims = ((1,), (0,))
+    sent = contract(parts, pair[0][...], dims) + contract(parts, pair[1][...], dims)
+    return jnp.sum(sent, axis=0, keepdims=True)
 
 
 def analysis_kernel(
@@ -201,10 +213,6 @@
     tiles = tiles_of(members)
     for t, (row, column) in enumerate(tiles):
         sys_ref[row : row + 8, column : column + 128] = sum_ref[t]
-    for i in range(blocks):
-        for j in range(i + 1, blocks):
-            upper = sys_ref[i * 128 : i * 128 + 128, j * 128 : j * 128 + 128]
-            sys_ref[j * 128 : j * 128 + 128, i * 128 : i * 128 + 128] = jnp.transpose(upper)
     tile = sum_ref[len(tiles) - 1]
     low_lanes = lax.broadcasted_iota(jnp.int32, (blocks, 128), 1) < 64
     projected = jnp.where(low_lanes, tile[0:blocks], pltpu.roll(tile[blocks : 2 * blocks], 64, 1))
@@ -212,16 +220,23 @@
     corner = sys_ref[members - 128 :, members - 128 :]
     low_lanes = lax.broadcasted_iota(jnp.int32, tile.shape, 1) < 64
     sys_ref[members - 8 :, members - 128 :] = jnp.where(low_lanes, jnp.transpose(corner)[120:128], tile)
-    row_iota = lax.broadcasted_iota(jnp.int32, (members, members), 0)
-    column_iota = lax.broadcasted_iota(jnp.int32, (members, members), 1)
-    diagonal = row_iota == column_iota
-    system = sys_ref[...] + jnp.where(diagonal, 1.0, 0.0)
-    squares = jnp.sum(jnp.sum(system * system, axis=0, keepdims=True), axis=1, keepdims=True)
+    squares = jnp.zeros((128, 128), F32)
+    unit = jnp.where(diagonal_of(128), 1.0, 0.0)
+    for i in range(blocks):
+        here = slice(i * 128, i * 128 + 128)
+        value = sys_ref[here, here] + unit
+        sys_ref[here, here] = value
+        squares = squares + value * value
+        for j in range(i + 1, blocks):
+            there = slice(j * 128, j * 128 + 128)
+            value = sys_ref[here, there]
+            sys_ref[there, here] = jnp.transpose(value)
+            squares = squares + 2.0 * (value * value)
+    squares = jnp.sum(jnp.sum(squares, axis=0, keepdims=True), axis=1, keepdims=True)
     norm_scale = jnp.sqrt(squares)
-    start_y = system / norm_scale
-
+    one_over = 1.0 / norm_scale
     half_size = members // 2
-    half_diagonal = diagonal[:half_size, :half_size]
+    half_diagonal = diagonal_of(half_size)
     y, z, t = (yh, yl), (zh, zl), (th, tl)
 
     def step_of(blocks):
@@ -229,8 +244,13 @@
         whole = jnp.where(half_diagonal, 1.5, 0.0)
         return whole - 0.5 * first, -0.5 * side, whole - 0.5 * last
 
-    zh[...], zl[...] = halves(jnp.where(diagonal, 1.5, 0.0) - 0.5 * start_y)
-    th[...], tl[...] = halves(start_y)
+    for r in (0, half_size):
+        for c in (0, half_size):
+            here = (slice(r, r + half_size), slice(c, c + half_size))
+            value = sys_ref[here] * one_over
+            th[here], tl[here] = halves(value)
+            base = jnp.where(half_diagonal, 1.5, 0.0) if r == c else 0.0
+            zh[here], zl[here] = halves(base - 0.5 * value)
     keep_product(y, product(z, t))
 
     def turn(_, carry):
@@ -242,19 +262,17 @@
 
     lax.fori_loop(0, NS_ITERS - 2, turn, 0, unroll=NS_ITERS - 2)
     keep_product(t, step_of(product(z, y)))
-    first, side, last = product(t, z)
-    sys_ref[:half_size, :half_size] = first
-    sys_ref[:half_size, half_size:] = side
-    sys_ref[half_size:, half_size:] = last
-    sys_ref[half_size:, :half_size] = jnp.transpose(side)
-    iterate_z = sys_ref[...]
     root = jnp.sqrt(norm_scale)
+    shift = through(through(projected, t), z) / (root * norm_factor)
+    first, side, last = (b * (1.0 / root) for b in product(t, z))
+    weights = jnp.concatenate(
+        [
+            jnp.concatenate([first, side], axis=1),
+            jnp.concatenate([jnp.transpose(side), last], axis=1),
+        ],
+        axis=0,
+    ).astype(BF16)
     dims = ((1,), (0,))
-    zs = halves(iterate_z)
-    three = thirds(projected)
-    sent = contract(three, zs[0], dims) + contract(three, zs[1], dims)
-    shift = jnp.sum(sent, axis=0, keepdims=True) / (root * norm_factor)
-    weights = (iterate_z / root).astype(BF16)
     combined = jnp.sum(contract(thirds(shift), weights, dims), axis=0, keepdims=True)
     combined = thirds(combined)
     groups, fields, rows, width = anomalies_ref.shape

time: 137 us -> 138 us (level)
  no operation moved by 1% of the time
where the time goes in v7:
time: 138 us; the launch traced here: 137 us
  blocking collectives  108 us (78%)
  Pallas kernels  23.2 us (17%)
  starting transfers between devices  4.38 us (3%)
  waiting for transfers between devices  1.67 us (1%)
    all_to_all x1, blocking collectives, local(): state = near(lax.all_to_all(packed, MEM, 0, 0, tiled=True))  37 us
    all_to_all x1, blocking collectives, local(): returned = lax.all_to_all(analysis, MEM, 0, 0, tiled=True)  31.6 us
    all_to_all x1, blocking collectives, local(): lax.all_to_all(spread(part, planes), 'cell', 0, 0, tiled=True)  16.4 us
    pallas_call x1, Pallas kernels, local(): pl.pallas_call(analysis_kernel, out_shape=tiled, in_specs=[SMEM, VMEM, VM...  16.3 us
    all_to_all x1, blocking collectives, local(): part = lax.all_to_all(part, PLANE, 0, 0, tiled=True)  12.2 us
    all_to_all x1, blocking collectives, local(): own = lax.all_to_all(spread(part, plane), PLANE, 0, 0, tiled=True)  10.6 us
    ppermute x1, starting transfers between devices, local(): other = lax.ppermute(own, 'mem_2', swap)  3.9 us
  transfers between devices with their start and end apart: 2, of which 2 were waited for; matrix products, arithmetic and copies ran while one was open for 0% of the time, Pallas kernels for 1%

profile of v7, /device:TPU:1, one launch (start us, length us, event | category | flops | bytes accessed | tf_op | source)
XLA Modules:
  0.0 137.4 jit_solution(2952656314628641541)
XLA Ops:
  0.0 2.5 %pack.1 = bf16[32,2,16,1024]{3,2,1,0:T(8,128)(2,1)} custom-call(bf16[16,2,32768]{2,1,0:T(2,128)(2,1)} %x_ref.1), custom_call_target="tpu_custom_call" | custom-call | tf_op jit(solution)/shard_map/pack/pallas_call | solution.py:312
  2.5 0.0 copy-start
  2.6 0.0 copy-start.1
  2.6 0.0 copy-start.2
  2.6 37.0 %all_to_all.25.x_ref = bf16[32,2,16,1024]{3,2,1,0:T(8,128)(2,1)S(1)} all-to-all(bf16[32,2,16,1024]{3,2,1,0:T(8,128)(2,1)} %pack.1), channel_id=1, replica_groups=mesh['mem_0'=4,'mem_1'=4,'mem_2'=2,'cell'=8] {'mem_0','mem_1','mem_2'}, dimensions={0} | all-to-all | bytes 4194304 | tf_op jit(solution)/shard_map/all_to_all | solution.py:325
  39.6 0.0 copy-done
  39.6 0.0 copy-done.1
  39.6 0.0 copy-done.2
  39.6 2.0 %gram.1 = (f32[80,8,128]{2,1,0:T(8,128)S(1)}, f32[80,8,128]{2,1,0:T(8,128)S(1)}) custom-call(s32[1]{0:T(128)} %bitcast.core_ref, s32[1]{0:T(128)} %bitcast.1.start_ref, s32[4,128]{1,0:T(4,128)S(1)} %copy-done, f32[4,128]{1,0:T(4,128)S(1)} %copy-done.1, f32[4,128]{1,0:T(4,128)S(1)} %copy-done.2, bf16[32,2,16,1024]{3,2,1,0:T(8,128)(2,1)S(1)} %all_to_all.25.x_ref), custom_call_target="tpu_custom_call" | custom-call | tf_op jit(solution)/shard_map/gram/pallas_call | solution.py:330
  41.6 0.5 collective-permute-start
  42.1 1.3 collective-permute-done
  43.4 12.2 %all_to_all.26 = f32[80,8,128]{2,1,0:T(8,128)S(1)} all-to-all(f32[80,8,128]{2,1,0:T(8,128)S(1)} %add.15), channel_id=1, replica_groups=mesh['mem_0'=4,'mem_1'=4,'mem_2'=2,'cell'=8] {'mem_0','mem_1'}, dimensions={0} | all-to-all | bytes 655360 | tf_op jit(solution)/shard_map/all_to_all | solution.py:341
  55.7 16.4 %all_to_all.27 = f32[40,8,128]{2,1,0:T(8,128)S(1)} all-to-all(f32[40,8,128]{2,1,0:T(8,128)S(1)} %bitcast.9), channel_id=1, replica_groups=mesh['mem_0'=4,'mem_1'=4,'mem_2'=2,'cell'=8] {'cell'}, dimensions={0} | all-to-all | bytes 327680 | tf_op jit(solution)/shard_map/all_to_all | solution.py:344
  72.1 10.6 %all_to_all.28.own_ref = f32[80,8,128]{2,1,0:T(8,128)S(1)} all-to-all(f32[80,8,128]{2,1,0:T(8,128)S(1)} %bitcast.7), channel_id=1, replica_groups=mesh['mem_0'=4,'mem_1'=4,'mem_2'=2,'cell'=8] {'mem_0','mem_1'}, dimensions={0} | all-to-all | bytes 655360 | tf_op jit(solution)/shard_map/all_to_all | solution.py:354
  82.7 3.9 %collective-permute-start.1 = (f32[80,8,128]{2,1,0:T(8,128)S(1)}, f32[80,8,128]{2,1,0:T(8,128)S(1)}, u32[]{:S(2)}, u32[]{:S(2)}) collective-permute-start(f32[80,8,128]{2,1,0:T(8,128)S(1)} %all_to_all.28.own_ref), channel_id=1, source_target_pairs={{0,8},{8,0},{1,9},{9,1},{2,10},{10,2},{3,11},{11,3},{4,12},{12,4},... | collective-permute-start | bytes 983048 | tf_op jit(solution)/shard_map/ppermute | solution.py:355
  86.6 0.8 mean.1
  87.5 0.4 collective-permute-done.1.other_ref
  87.9 16.3 %analysis.1 = bf16[32,2,16,1024]{3,2,1,0:T(8,128)(2,1)S(1)} custom-call(s32[1]{0:T(128)} %bitcast.core_ref, f32[80,8,128]{2,1,0:T(8,128)S(1)} %all_to_all.28.own_ref, f32[80,8,128]{2,1,0:T(8,128)S(1)} %collective-permute-done.1.other_ref, bf16[32,2,16,1024]{3,2,1,0:T(8,128)(2,1)S(1)} %get-tuple-element.17.anomalies_ref, f32[2,1024]{1,0:T(2,128)S(1)} %get-tuple-element.18.mean_ref), custom_call_target="tpu_custom_call" | custom-call | tf_op jit(solution)/shard_map/analysis/pallas_call | solution.py:358
  104.2 31.6 %all_to_all.29.y_ref = bf16[32,2,16,1024]{3,2,1,0:T(8,128)(2,1)S(1)} all-to-all(bf16[32,2,16,1024]{3,2,1,0:T(8,128)(2,1)S(1)} %analysis.1), channel_id=1, replica_groups=mesh['mem_0'=4,'mem_1'=4,'mem_2'=2,'cell'=8] {'mem_0','mem_1','mem_2'}, dimensions={0} | all-to-all | bytes 4194304 | tf_op jit(solution)/shard_map/all_to_all | solution.py:367
  135.8 1.4 %unpack.1 = bf16[16,2,32768]{2,1,0:T(2,128)(2,1)} custom-call(bf16[32,2,16,1024]{3,2,1,0:T(8,128)(2,1)S(1)} %all_to_all.29.y_ref), custom_call_target="tpu_custom_call" | custom-call | tf_op jit(solution)/shard_map/unpack/pallas_call | solution.py:368
  (5 shorter events, 0.1 us)
Async XLA Ops:
  2.5 37.0 %copy-start = (s32[4,128]{1,0:T(4,128)S(1)}, s32[4,128]{1,0:T(4,128)}, u32[]{:S(2)}) copy-start(s32[4,128]{1,0:T(4,128)} %location_ref.1) | copy-start | bytes 6148
  2.6 37.0 %copy-start.1 = (f32[4,128]{1,0:T(4,128)S(1)}, f32[4,128]{1,0:T(4,128)}, u32[]{:S(2)}) copy-start(f32[4,128]{1,0:T(4,128)} %datum_ref.1) | copy-start | bytes 6148
  2.6 37.0 %copy-start.2 = (f32[4,128]{1,0:T(4,128)S(1)}, f32[4,128]{1,0:T(4,128)}, u32[]{:S(2)}) copy-start(f32[4,128]{1,0:T(4,128)} %spread_ref.1) | copy-start | bytes 6148
  41.6 1.7 %collective-permute-start = (f32[80,8,128]{2,1,0:T(8,128)S(1)}, f32[80,8,128]{2,1,0:T(8,128)S(1)}, u32[]{:S(2)}, u32[]{:S(2)}) collective-permute-start(f32[80,8,128]{2,1,0:T(8,128)S(1)} %get-tuple-element.16), channel_id=1, source_target_pairs={{0,8},{8,0},{1,9},{9,1},{2,10},{10,2},{3,11},{11,3},{4,12},{12,4},... | collective-permute-start | bytes 983048 | tf_op jit(solution)/shard_map/ppermute | solution.py:340
  82.7 5.2 %collective-permute-start.1 = (f32[80,8,128]{2,1,0:T(8,128)S(1)}, f32[80,8,128]{2,1,0:T(8,128)S(1)}, u32[]{:S(2)}, u32[]{:S(2)}) collective-permute-start(f32[80,8,128]{2,1,0:T(8,128)S(1)} %all_to_all.28.own_ref), channel_id=1, source_target_pairs={{0,8},{8,0},{1,9},{9,1},{2,10},{10,2},{3,11},{11,3},{4,12},{12,4},... | collective-permute-start | bytes 983048 | tf_op jit(solution)/shard_map/ppermute | solution.py:355

commit v8 on v7

--- a/solution.py
+++ b/solution.py
@@ -187,6 +187,38 @@
     return jnp.sum(sent, axis=0, keepdims=True)
 
 
+def keep_step(rest_ref, scale_ref, blocks):
+    half = rest_ref.shape[0] // 2
+    first, side, last = blocks
+    diagonal = diagonal_of(half)
+    for start, value in ((0, first), (half, last)):
+        value = jnp.where(diagonal, 1.5, 0.0) - 0.5 * value
+        scale = jnp.sum(jnp.where(diagonal, value, 0.0), axis=1, keepdims=True)
+        scale_ref[start : start + half, :] = jnp.broadcast_to(scale, (half, scale_ref.shape[1]))
+        rest = jnp.where(diagonal, 0.0, value).astype(BF16)
+        rest_ref[start : start + half, start : start + half] = rest
+    side = -0.5 * side
+    rest_ref[:half, half:] = side.astype(BF16)
+    rest_ref[half:, :half] = jnp.transpose(side).astype(BF16)
+
+
+def stepped(rest_ref, scale_ref, pair):
+    half = rest_ref.shape[0] // 2
+    high_ref, low_ref = pair
+    dims = ((1,), (0,))
+
+    def block(r, c):
+        rows, columns = slice(r, r + half), slice(c, c + half)
+        scale = scale_ref[rows, :]
+        scale = jnp.concatenate([scale] * (half // scale.shape[1]), axis=1)
+        value = high_ref[rows, columns].astype(F32) + low_ref[rows, columns].astype(F32)
+        rest = rest_ref[rows, :]
+        moved = contract(rest, high_ref[:, columns], dims) + contract(rest, low_ref[:, columns], dims)
+        return scale * value + moved
+
+    return block(0, 0), block(0, half), block(half, half)
+
+
 def analysis_kernel(
     core_ref,
     own_ref,
@@ -202,6 +234,7 @@
     zl,
     th,
     tl,
+    scale_ref,
 ):
     members = sys_ref.shape[0]
     norm_factor = math.sqrt(members - 1)
@@ -239,11 +272,6 @@
     half_diagonal = diagonal_of(half_size)
     y, z, t = (yh, yl), (zh, zl), (th, tl)
 
-    def step_of(blocks):
-        first, side, last = blocks
-        whole = jnp.where(half_diagonal, 1.5, 0.0)
-        return whole - 0.5 * first, -0.5 * side, whole - 0.5 * last
-
     for r in (0, half_size):
         for c in (0, half_size):
             here = (slice(r, r + half_size), slice(c, c + half_size))
@@ -254,25 +282,27 @@
     keep_product(y, product(z, t))
 
     def turn(_, carry):
-        keep_product(t, step_of(product(z, y)))
-        next_y, next_z = product(t, y), product(t, z)
+        keep_step(th, scale_ref, product(z, y))
+        next_y, next_z = stepped(th, scale_ref, y), stepped(th, scale_ref, z)
         keep_product(y, next_y)
         keep_product(z, next_z)
         return carry
 
     lax.fori_loop(0, NS_ITERS - 2, turn, 0, unroll=NS_ITERS - 2)
-    keep_product(t, step_of(product(z, y)))
+    keep_step(th, scale_ref, product(z, y))
+    first, side, last = stepped(th, scale_ref, z)
+    sys_ref[:half_size, :half_size] = first
+    sys_ref[:half_size, half_size:] = side
+    sys_ref[half_size:, half_size:] = last
+    sys_ref[half_size:, :half_size] = jnp.transpose(side)
+    iterate_z = sys_ref[...]
     root = jnp.sqrt(norm_scale)
-    shift = through(through(projected, t), z) / (root * norm_factor)
-    first, side, last = (b * (1.0 / root) for b in product(t, z))
-    weights = jnp.concatenate(
-        [
-            jnp.concatenate([first, side], axis=1),
-            jnp.concatenate([jnp.transpose(side), last], axis=1),
-        ],
-        axis=0,
-    ).astype(BF16)
     dims = ((1,), (0,))
+    zs = halves(iterate_z)
+    three = thirds(projected)
+    sent = contract(three, zs[0], dims) + contract(three, zs[1], dims)
+    shift = jnp.sum(sent, axis=0, keepdims=True) / (root * norm_factor)
+    weights = (iterate_z * (1.0 / root)).astype(BF16)
     combined = jnp.sum(contract(thirds(shift), weights, dims), axis=0, keepdims=True)
     combined = thirds(combined)
     groups, fields, rows, width = anomalies_ref.shape
@@ -360,7 +390,7 @@
         out_shape=tiled,
         in_specs=[SMEM, VMEM, VMEM, VMEM, VMEM],
         out_specs=VMEM,
-        scratch_shapes=[both, whole] + [square] * 6,
+        scratch_shapes=[both, whole] + [square] * 6 + [pltpu.VMEM((members, 128), F32)],
         compiler_params=pltpu.CompilerParams(vmem_limit_bytes=32 << 20),
         name="analysis",
     )(core, near(own), near(other), near(anomalies), near(mean))

time: 138 us -> 135 us (0.978)
  Pallas kernels: 23.2 us -> 20.2 us
    pallas_call x1, Pallas kernels: 16.3 us -> 13.3 us  [local(): pl.pallas_call(analysis_kernel, out_shape=tiled, in_specs=[SMEM, VMEM, VM...]
where the time goes in v8:
time: 135 us; the launch traced here: 134 us
  blocking collectives  108 us (80%)
  Pallas kernels  20.2 us (15%)
  starting transfers between devices  4.38 us (3%)
  waiting for transfers between devices  1.67 us (1%)
    all_to_all x1, blocking collectives, local(): state = near(lax.all_to_all(packed, MEM, 0, 0, tiled=True))  37 us
    all_to_all x1, blocking collectives, local(): returned = lax.all_to_all(analysis, MEM, 0, 0, tiled=True)  31.6 us
    all_to_all x1, blocking collectives, local(): lax.all_to_all(spread(part, planes), 'cell', 0, 0, tiled=True)  16.4 us
    pallas_call x1, Pallas kernels, local(): pl.pallas_call(analysis_kernel, out_shape=tiled, in_specs=[SMEM, VMEM, VM...  13.3 us
    all_to_all x1, blocking collectives, local(): part = lax.all_to_all(part, PLANE, 0, 0, tiled=True)  12.2 us
    all_to_all x1, blocking collectives, local(): own = lax.all_to_all(spread(part, plane), PLANE, 0, 0, tiled=True)  10.6 us
    ppermute x1, starting transfers between devices, local(): other = lax.ppermute(own, 'mem_2', swap)  3.9 us
  transfers between devices with their start and end apart: 2, of which 2 were waited for; matrix products, arithmetic and copies ran while one was open for 0% of the time, Pallas kernels for 1%

profile of v8, /device:TPU:1, one launch (start us, length us, event | category | flops | bytes accessed | tf_op | source)
XLA Modules:
  0.0 134.4 jit_solution(8223334842613975398)
XLA Ops:
  0.0 2.5 %pack.1 = bf16[32,2,16,1024]{3,2,1,0:T(8,128)(2,1)} custom-call(bf16[16,2,32768]{2,1,0:T(2,128)(2,1)} %x_ref.1), custom_call_target="tpu_custom_call" | custom-call | tf_op jit(solution)/shard_map/pack/pallas_call | solution.py:342
  2.5 0.0 copy-start
  2.6 0.0 copy-start.1
  2.6 0.0 copy-start.2
  2.6 37.0 %all_to_all.25.x_ref = bf16[32,2,16,1024]{3,2,1,0:T(8,128)(2,1)S(1)} all-to-all(bf16[32,2,16,1024]{3,2,1,0:T(8,128)(2,1)} %pack.1), channel_id=1, replica_groups=mesh['mem_0'=4,'mem_1'=4,'mem_2'=2,'cell'=8] {'mem_0','mem_1','mem_2'}, dimensions={0} | all-to-all | bytes 4194304 | tf_op jit(solution)/shard_map/all_to_all | solution.py:355
  39.6 0.0 copy-done
  39.6 0.0 copy-done.1
  39.6 0.0 copy-done.2
  39.6 2.0 %gram.1 = (f32[80,8,128]{2,1,0:T(8,128)S(1)}, f32[80,8,128]{2,1,0:T(8,128)S(1)}) custom-call(s32[1]{0:T(128)} %bitcast.core_ref, s32[1]{0:T(128)} %bitcast.1.start_ref, s32[4,128]{1,0:T(4,128)S(1)} %copy-done, f32[4,128]{1,0:T(4,128)S(1)} %copy-done.1, f32[4,128]{1,0:T(4,128)S(1)} %copy-done.2, bf16[32,2,16,1024]{3,2,1,0:T(8,128)(2,1)S(1)} %all_to_all.25.x_ref), custom_call_target="tpu_custom_call" | custom-call | tf_op jit(solution)/shard_map/gram/pallas_call | solution.py:360
  41.6 0.5 collective-permute-start
  42.1 1.3 collective-permute-done
  43.4 12.2 %all_to_all.26 = f32[80,8,128]{2,1,0:T(8,128)S(1)} all-to-all(f32[80,8,128]{2,1,0:T(8,128)S(1)} %add.15), channel_id=1, replica_groups=mesh['mem_0'=4,'mem_1'=4,'mem_2'=2,'cell'=8] {'mem_0','mem_1'}, dimensions={0} | all-to-all | bytes 655360 | tf_op jit(solution)/shard_map/all_to_all | solution.py:371
  55.7 16.4 %all_to_all.27 = f32[40,8,128]{2,1,0:T(8,128)S(1)} all-to-all(f32[40,8,128]{2,1,0:T(8,128)S(1)} %bitcast.9), channel_id=1, replica_groups=mesh['mem_0'=4,'mem_1'=4,'mem_2'=2,'cell'=8] {'cell'}, dimensions={0} | all-to-all | bytes 327680 | tf_op jit(solution)/shard_map/all_to_all | solution.py:374
  72.1 10.6 %all_to_all.28.own_ref = f32[80,8,128]{2,1,0:T(8,128)S(1)} all-to-all(f32[80,8,128]{2,1,0:T(8,128)S(1)} %bitcast.7), channel_id=1, replica_groups=mesh['mem_0'=4,'mem_1'=4,'mem_2'=2,'cell'=8] {'mem_0','mem_1'}, dimensions={0} | all-to-all | bytes 655360 | tf_op jit(solution)/shard_map/all_to_all | solution.py:384
  82.7 3.9 %collective-permute-start.1 = (f32[80,8,128]{2,1,0:T(8,128)S(1)}, f32[80,8,128]{2,1,0:T(8,128)S(1)}, u32[]{:S(2)}, u32[]{:S(2)}) collective-permute-start(f32[80,8,128]{2,1,0:T(8,128)S(1)} %all_to_all.28.own_ref), channel_id=1, source_target_pairs={{0,8},{8,0},{1,9},{9,1},{2,10},{10,2},{3,11},{11,3},{4,12},{12,4},... | collective-permute-start | bytes 983048 | tf_op jit(solution)/shard_map/ppermute | solution.py:385
  86.6 0.8 mean.1
  87.5 0.4 collective-permute-done.1.other_ref
  87.9 13.3 %analysis.1 = bf16[32,2,16,1024]{3,2,1,0:T(8,128)(2,1)S(1)} custom-call(s32[1]{0:T(128)} %bitcast.core_ref, f32[80,8,128]{2,1,0:T(8,128)S(1)} %all_to_all.28.own_ref, f32[80,8,128]{2,1,0:T(8,128)S(1)} %collective-permute-done.1.other_ref, bf16[32,2,16,1024]{3,2,1,0:T(8,128)(2,1)S(1)} %get-tuple-element.17.anomalies_ref, f32[2,1024]{1,0:T(2,128)S(1)} %get-tuple-element.18.mean_ref), custom_call_target="tpu_custom_call" | custom-call | tf_op jit(solution)/shard_map/analysis/pallas_call | solution.py:388
  101.2 31.6 %all_to_all.29.y_ref = bf16[32,2,16,1024]{3,2,1,0:T(8,128)(2,1)S(1)} all-to-all(bf16[32,2,16,1024]{3,2,1,0:T(8,128)(2,1)S(1)} %analysis.1), channel_id=1, replica_groups=mesh['mem_0'=4,'mem_1'=4,'mem_2'=2,'cell'=8] {'mem_0','mem_1','mem_2'}, dimensions={0} | all-to-all | bytes 4194304 | tf_op jit(solution)/shard_map/all_to_all | solution.py:397
  132.8 1.4 %unpack.1 = bf16[16,2,32768]{2,1,0:T(2,128)(2,1)} custom-call(bf16[32,2,16,1024]{3,2,1,0:T(8,128)(2,1)S(1)} %all_to_all.29.y_ref), custom_call_target="tpu_custom_call" | custom-call | tf_op jit(solution)/shard_map/unpack/pallas_call | solution.py:398
  (5 shorter events, 0.1 us)
Async XLA Ops:
  2.5 37.0 %copy-start = (s32[4,128]{1,0:T(4,128)S(1)}, s32[4,128]{1,0:T(4,128)}, u32[]{:S(2)}) copy-start(s32[4,128]{1,0:T(4,128)} %location_ref.1) | copy-start | bytes 6148
  2.6 37.0 %copy-start.1 = (f32[4,128]{1,0:T(4,128)S(1)}, f32[4,128]{1,0:T(4,128)}, u32[]{:S(2)}) copy-start(f32[4,128]{1,0:T(4,128)} %datum_ref.1) | copy-start | bytes 6148
  2.6 37.0 %copy-start.2 = (f32[4,128]{1,0:T(4,128)S(1)}, f32[4,128]{1,0:T(4,128)}, u32[]{:S(2)}) copy-start(f32[4,128]{1,0:T(4,128)} %spread_ref.1) | copy-start | bytes 6148
  41.6 1.7 %collective-permute-start = (f32[80,8,128]{2,1,0:T(8,128)S(1)}, f32[80,8,128]{2,1,0:T(8,128)S(1)}, u32[]{:S(2)}, u32[]{:S(2)}) collective-permute-start(f32[80,8,128]{2,1,0:T(8,128)S(1)} %get-tuple-element.16), channel_id=1, source_target_pairs={{0,8},{8,0},{1,9},{9,1},{2,10},{10,2},{3,11},{11,3},{4,12},{12,4},... | collective-permute-start | bytes 983048 | tf_op jit(solution)/shard_map/ppermute | solution.py:370
  82.7 5.2 %collective-permute-start.1 = (f32[80,8,128]{2,1,0:T(8,128)S(1)}, f32[80,8,128]{2,1,0:T(8,128)S(1)}, u32[]{:S(2)}, u32[]{:S(2)}) collective-permute-start(f32[80,8,128]{2,1,0:T(8,128)S(1)} %all_to_all.28.own_ref), channel_id=1, source_target_pairs={{0,8},{8,0},{1,9},{9,1},{2,10},{10,2},{3,11},{11,3},{4,12},{12,4},... | collective-permute-start | bytes 983048 | tf_op jit(solution)/shard_map/ppermute | solution.py:385

commit v9 on v8

--- a/solution.py
+++ b/solution.py
@@ -305,13 +305,15 @@
     weights = (iterate_z * (1.0 / root)).astype(BF16)
     combined = jnp.sum(contract(thirds(shift), weights, dims), axis=0, keepdims=True)
     combined = thirds(combined)
+    weights = jnp.concatenate([combined, weights], axis=0)
     groups, fields, rows, width = anomalies_ref.shape
     for f in range(fields):
         anomalies = rows_of(anomalies_ref, f)
-        mean_shift = jnp.sum(contract(combined, anomalies, dims), axis=0, keepdims=True)
+        moved = contract(weights, anomalies, dims)
+        extra = combined.shape[0]
+        mean_shift = jnp.sum(moved[:extra], axis=0, keepdims=True)
         base = mean_ref[f : f + 1, :] + mean_shift
-        updated = contract(weights, anomalies, dims)
-        o_ref[:, f] = (base + updated).astype(BF16).reshape(groups, rows, width)
+        o_ref[:, f] = (base + moved[extra:]).astype(BF16).reshape(groups, rows, width)
 
 
 def far(a):
@@ -336,7 +338,7 @@
     members = rows * peers
     width = span // peers
     core = lax.axis_index("mem_2").reshape(1).astype(jnp.int32)
-    parts = 4
+    parts = 8
     staging = [pltpu.VMEM((parts, rows, fields, span // parts), BF16), pltpu.SemaphoreType.DMA((parts,))]
     tiled = pltpu.VMEM((peers, fields, rows, width), BF16)
     packed = pl.pallas_call(

time: 135 us -> 135 us (level)
  no operation moved by 1% of the time
where the time goes in v9:
time: 135 us; the launch traced here: 134 us
  blocking collectives  108 us (80%)
  Pallas kernels  20 us (15%)
  starting transfers between devices  4.39 us (3%)
  waiting for transfers between devices  1.67 us (1%)
    all_to_all x1, blocking collectives, local(): state = near(lax.all_to_all(packed, MEM, 0, 0, tiled=True))  37 us
    all_to_all x1, blocking collectives, local(): returned = lax.all_to_all(analysis, MEM, 0, 0, tiled=True)  31.6 us
    all_to_all x1, blocking collectives, local(): lax.all_to_all(spread(part, planes), 'cell', 0, 0, tiled=True)  16.4 us
    pallas_call x1, Pallas kernels, local(): pl.pallas_call(analysis_kernel, out_shape=tiled, in_specs=[SMEM, VMEM, VM...  13.2 us
    all_to_all x1, blocking collectives, local(): part = lax.all_to_all(part, PLANE, 0, 0, tiled=True)  12.2 us
    all_to_all x1, blocking collectives, local(): own = lax.all_to_all(spread(part, plane), PLANE, 0, 0, tiled=True)  10.6 us
    ppermute x1, starting transfers between devices, local(): other = lax.ppermute(own, 'mem_2', swap)  3.9 us
  transfers between devices with their start and end apart: 2, of which 2 were waited for; matrix products, arithmetic and copies ran while one was open for 0% of the time, Pallas kernels for 1%

profile of v9, /device:TPU:1, one launch (start us, length us, event | category | flops | bytes accessed | tf_op | source)
XLA Modules:
  0.0 134.2 jit_solution(5199917804534993191)
XLA Ops:
  0.0 2.4 %pack.1 = bf16[32,2,16,1024]{3,2,1,0:T(8,128)(2,1)} custom-call(bf16[16,2,32768]{2,1,0:T(2,128)(2,1)} %x_ref.1), custom_call_target="tpu_custom_call" | custom-call | tf_op jit(solution)/shard_map/pack/pallas_call | solution.py:344
  2.5 0.0 copy-start
  2.5 0.0 copy-start.1
  2.5 0.0 copy-start.2
  2.5 37.0 %all_to_all.25.x_ref = bf16[32,2,16,1024]{3,2,1,0:T(8,128)(2,1)S(1)} all-to-all(bf16[32,2,16,1024]{3,2,1,0:T(8,128)(2,1)} %pack.1), channel_id=1, replica_groups=mesh['mem_0'=4,'mem_1'=4,'mem_2'=2,'cell'=8] {'mem_0','mem_1','mem_2'}, dimensions={0} | all-to-all | bytes 4194304 | tf_op jit(solution)/shard_map/all_to_all | solution.py:357
  39.5 0.0 copy-done
  39.5 0.0 copy-done.1
  39.5 0.0 copy-done.2
  39.5 2.0 %gram.1 = (f32[80,8,128]{2,1,0:T(8,128)S(1)}, f32[80,8,128]{2,1,0:T(8,128)S(1)}) custom-call(s32[1]{0:T(128)} %bitcast.core_ref, s32[1]{0:T(128)} %bitcast.1.start_ref, s32[4,128]{1,0:T(4,128)S(1)} %copy-done, f32[4,128]{1,0:T(4,128)S(1)} %copy-done.1, f32[4,128]{1,0:T(4,128)S(1)} %copy-done.2, bf16[32,2,16,1024]{3,2,1,0:T(8,128)(2,1)S(1)} %all_to_all.25.x_ref), custom_call_target="tpu_custom_call" | custom-call | tf_op jit(solution)/shard_map/gram/pallas_call | solution.py:362
  41.6 0.5 collective-permute-start
  42.1 1.3 collective-permute-done
  43.4 12.2 %all_to_all.26 = f32[80,8,128]{2,1,0:T(8,128)S(1)} all-to-all(f32[80,8,128]{2,1,0:T(8,128)S(1)} %add.15), channel_id=1, replica_groups=mesh['mem_0'=4,'mem_1'=4,'mem_2'=2,'cell'=8] {'mem_0','mem_1'}, dimensions={0} | all-to-all | bytes 655360 | tf_op jit(solution)/shard_map/all_to_all | solution.py:373
  55.6 16.4 %all_to_all.27 = f32[40,8,128]{2,1,0:T(8,128)S(1)} all-to-all(f32[40,8,128]{2,1,0:T(8,128)S(1)} %bitcast.9), channel_id=1, replica_groups=mesh['mem_0'=4,'mem_1'=4,'mem_2'=2,'cell'=8] {'cell'}, dimensions={0} | all-to-all | bytes 327680 | tf_op jit(solution)/shard_map/all_to_all | solution.py:376
  72.0 10.6 %all_to_all.28.own_ref = f32[80,8,128]{2,1,0:T(8,128)S(1)} all-to-all(f32[80,8,128]{2,1,0:T(8,128)S(1)} %bitcast.7), channel_id=1, replica_groups=mesh['mem_0'=4,'mem_1'=4,'mem_2'=2,'cell'=8] {'mem_0','mem_1'}, dimensions={0} | all-to-all | bytes 655360 | tf_op jit(solution)/shard_map/all_to_all | solution.py:386
  82.6 3.9 %collective-permute-start.1 = (f32[80,8,128]{2,1,0:T(8,128)S(1)}, f32[80,8,128]{2,1,0:T(8,128)S(1)}, u32[]{:S(2)}, u32[]{:S(2)}) collective-permute-start(f32[80,8,128]{2,1,0:T(8,128)S(1)} %all_to_all.28.own_ref), channel_id=1, source_target_pairs={{0,8},{8,0},{1,9},{9,1},{2,10},{10,2},{3,11},{11,3},{4,12},{12,4},... | collective-permute-start | bytes 983048 | tf_op jit(solution)/shard_map/ppermute | solution.py:387
  86.5 0.8 mean.1
  87.4 0.4 collective-permute-done.1.other_ref
  87.8 13.2 %analysis.1 = bf16[32,2,16,1024]{3,2,1,0:T(8,128)(2,1)S(1)} custom-call(s32[1]{0:T(128)} %bitcast.core_ref, f32[80,8,128]{2,1,0:T(8,128)S(1)} %all_to_all.28.own_ref, f32[80,8,128]{2,1,0:T(8,128)S(1)} %collective-permute-done.1.other_ref, bf16[32,2,16,1024]{3,2,1,0:T(8,128)(2,1)S(1)} %get-tuple-element.17.anomalies_ref, f32[2,1024]{1,0:T(2,128)S(1)} %get-tuple-element.18.mean_ref), custom_call_target="tpu_custom_call" | custom-call | tf_op jit(solution)/shard_map/analysis/pallas_call | solution.py:390
  101.0 31.6 %all_to_all.29.y_ref = bf16[32,2,16,1024]{3,2,1,0:T(8,128)(2,1)S(1)} all-to-all(bf16[32,2,16,1024]{3,2,1,0:T(8,128)(2,1)S(1)} %analysis.1), channel_id=1, replica_groups=mesh['mem_0'=4,'mem_1'=4,'mem_2'=2,'cell'=8] {'mem_0','mem_1','mem_2'}, dimensions={0} | all-to-all | bytes 4194304 | tf_op jit(solution)/shard_map/all_to_all | solution.py:399
  132.6 1.4 %unpack.1 = bf16[16,2,32768]{2,1,0:T(2,128)(2,1)} custom-call(bf16[32,2,16,1024]{3,2,1,0:T(8,128)(2,1)S(1)} %all_to_all.29.y_ref), custom_call_target="tpu_custom_call" | custom-call | tf_op jit(solution)/shard_map/unpack/pallas_call | solution.py:400
  (5 shorter events, 0.1 us)
Async XLA Ops:
  2.5 37.0 %copy-start = (s32[4,128]{1,0:T(4,128)S(1)}, s32[4,128]{1,0:T(4,128)}, u32[]{:S(2)}) copy-start(s32[4,128]{1,0:T(4,128)} %location_ref.1) | copy-start | bytes 6148
  2.5 37.0 %copy-start.1 = (f32[4,128]{1,0:T(4,128)S(1)}, f32[4,128]{1,0:T(4,128)}, u32[]{:S(2)}) copy-start(f32[4,128]{1,0:T(4,128)} %datum_ref.1) | copy-start | bytes 6148
  2.5 37.0 %copy-start.2 = (f32[4,128]{1,0:T(4,128)S(1)}, f32[4,128]{1,0:T(4,128)}, u32[]{:S(2)}) copy-start(f32[4,128]{1,0:T(4,128)} %spread_ref.1) | copy-start | bytes 6148
  41.6 1.7 %collective-permute-start = (f32[80,8,128]{2,1,0:T(8,128)S(1)}, f32[80,8,128]{2,1,0:T(8,128)S(1)}, u32[]{:S(2)}, u32[]{:S(2)}) collective-permute-start(f32[80,8,128]{2,1,0:T(8,128)S(1)} %get-tuple-element.16), channel_id=1, source_target_pairs={{0,8},{8,0},{1,9},{9,1},{2,10},{10,2},{3,11},{11,3},{4,12},{12,4},... | collective-permute-start | bytes 983048 | tf_op jit(solution)/shard_map/ppermute | solution.py:372
  82.6 5.2 %collective-permute-start.1 = (f32[80,8,128]{2,1,0:T(8,128)S(1)}, f32[80,8,128]{2,1,0:T(8,128)S(1)}, u32[]{:S(2)}, u32[]{:S(2)}) collective-permute-start(f32[80,8,128]{2,1,0:T(8,128)S(1)} %all_to_all.28.own_ref), channel_id=1, source_target_pairs={{0,8},{8,0},{1,9},{9,1},{2,10},{10,2},{3,11},{11,3},{4,12},{12,4},... | collective-permute-start | bytes 983048 | tf_op jit(solution)/shard_map/ppermute | solution.py:387
